TPU v7x, 32 devices: a whole 2x2x4 slice. The times are simulated.
32 devices in a mesh: slot: 8 (over z, x), grp: 4 (over y, core).
Axes of the slice: x: 2, y: 2, z: 4, core: 2. Of those that a mesh axis runs over, the one named last changes fastest.
Arguments:
- token_rows: bfloat16 [2, 8, 4, 384, 2048], P(None, 'slot', 'grp'), may hold values from -6 to 6
- cotangents: bfloat16 [2, 8, 4, 384, 2048], P(None, 'slot', 'grp'), may hold values from -6 to 6
- row_counts: int32 [2, 8, 4], P(None, 'slot', 'grp'), may hold values from 96 to 384, as said below
- old_place: int32 [8, 4], replicated, may hold values from 0 to 3, as said below
- new_place: int32 [8, 4], replicated, may hold values from 0 to 3, as said below
- momentum: float32 [16, 3145728], P(None, ('slot', 'grp')), may hold values from -4 to 4
- curvature: float32 [16, 3145728], P(None, ('slot', 'grp')), may hold values from 0.01 to 1
- master: float32 [16, 3145728], P(None, ('slot', 'grp')), may hold values from -0.125 to 0.125
Outputs:
- d_rows: bfloat16 [2, 8, 4, 384, 2048], P(None, 'slot', 'grp')
- momentum_out: float32 [16, 3145728], P(None, ('slot', 'grp'))
- curvature_out: float32 [16, 3145728], P(None, ('slot', 'grp'))
- master_out: float32 [16, 3145728], P(None, ('slot', 'grp'))
Inputs may be any that keep to these rules, and one draw needn't show every extreme that they name: `old_place`: entry [s, g] is the expert, numbered within group g, held by slot s of group g; each of the 4 experts of every group has at least one slot. `new_place`: entry [s, g] is the expert, numbered within group g, held by slot s of group g; each of the 4 experts of every group has at least one slot. `row_counts`: rows from this count on are padding; in each step some slot has exactly 384 live rows.
All inputs are finite; a program needn't handle non-finite values.
Results may differ from a plain program's by a relative error of at most 0.0074.
Values may be sent and summed in bfloat16 or wider, within the bound.
A program may use at most 128 MiB of HBM per device.

v0:
```python
import jax
import jax.numpy as jnp
from jax import lax
from jax.sharding import PartitionSpec as P

D = 2048
FF = 512


beta_one = 0.9
beta_two = 0.99
rho_scale = 2.0
learn_rate = 0.005
grad_scale = 0.25


def silu_parts(values):
    sigmoid = jax.nn.sigmoid(values)
    return (values * sigmoid, sigmoid * (1.0 + values * (1.0 - sigmoid)))


def slot_backward(rows_one, cotangent, live_count, flat_weights):
    split_at = 2 * D * FF
    w_gateup = flat_weights[:split_at].reshape(D, 2 * FF)
    w_down = flat_weights[split_at:].reshape(FF, D)
    live = (jnp.arange(rows_one.shape[0], dtype=jnp.int32) < live_count)[:, None]
    masked_ct = jnp.where(live, cotangent, jnp.zeros_like(cotangent))
    preact = jnp.dot(rows_one, w_gateup, preferred_element_type=jnp.float32)
    gate_pre = preact[:, :FF]
    up_pre = preact[:, FF:]
    activated, slope = silu_parts(gate_pre)
    hidden = (activated * up_pre).astype(jnp.bfloat16)
    hidden_grad = lax.dot_general(
        masked_ct, w_down, (((1,), (1,)), ((), ())), preferred_element_type=jnp.float32
    )
    pre_grad = jnp.concatenate(
        [hidden_grad * up_pre * slope, hidden_grad * activated], axis=1
    ).astype(jnp.bfloat16)
    row_grad = lax.dot_general(
        pre_grad, w_gateup, (((1,), (1,)), ((), ())), preferred_element_type=jnp.float32
    ).astype(jnp.bfloat16)
    grad_gateup = lax.dot_general(
        rows_one, pre_grad, (((0,), (0,)), ((), ())), preferred_element_type=jnp.float32
    )
    grad_down = lax.dot_general(
        hidden, masked_ct, (((0,), (0,)), ((), ())), preferred_element_type=jnp.float32
    )
    return (row_grad, jnp.concatenate([grad_gateup.reshape(-1), grad_down.reshape(-1)]))


def sophia(grads, momentum, curvature, master):
    momentum = beta_one * momentum + (1.0 - beta_one) * grads
    curvature = beta_two * curvature + (1.0 - beta_two) * grads * grads
    master = master - learn_rate * jnp.clip(momentum / (rho_scale * curvature), -1.0, 1.0)
    return (momentum, curvature, master)


def body(token_rows, cotangents, row_counts, old_place, new_place, momentum, curvature, master):
    group_count = lax.axis_size("grp")
    slot_count = lax.axis_size("slot")
    device_count = group_count * slot_count
    experts = master.shape[0]
    per_group = experts // group_count
    shard_len = master.shape[1]
    owners = (jnp.arange(group_count, dtype=jnp.int32) * per_group)[None, :]
    outputs = []
    for step_index, place_map in ((0, old_place), (1, new_place)):
        weights_bf = master.astype(jnp.bfloat16)
        send_expert_ids = (place_map + owners).reshape(-1)
        outgoing = jnp.take(weights_bf, send_expert_ids, axis=0)
        send_arrived = lax.all_to_all(
            outgoing, ("slot", "grp"), split_axis=0, concat_axis=0, tiled=True
        )
        slot_weights = send_arrived.reshape(-1)
        row_grad, flat_grad = slot_backward(
            token_rows[step_index, 0, 0],
            cotangents[step_index, 0, 0],
            row_counts[step_index, 0, 0],
            slot_weights,
        )
        arrived = lax.all_to_all(
            flat_grad.reshape(device_count, shard_len),
            ("slot", "grp"),
            split_axis=0,
            concat_axis=0,
            tiled=True,
        )
        expert_ids = (place_map + owners).reshape(-1)
        selector = (expert_ids[None, :] == jnp.arange(experts, dtype=jnp.int32)[:, None]).astype(
            jnp.float32
        )
        totals = jnp.dot(
            selector, arrived, precision=lax.Precision.HIGHEST, preferred_element_type=jnp.float32
        )
        grads = totals * grad_scale
        momentum, curvature, master = sophia(grads, momentum, curvature, master)
        outputs.append(row_grad)
    return (jnp.stack(outputs)[:, None, None], momentum, curvature, master)


def solution(mesh):
    return jax.shard_map(
        body,
        mesh=mesh,
        in_specs=(
            P(None, "slot", "grp", None, None),
            P(None, "slot", "grp", None, None),
            P(None, "slot", "grp"),
            P(),
            P(),
            P(None, ("slot", "grp")),
            P(None, ("slot", "grp")),
            P(None, ("slot", "grp")),
        ),
        out_specs=(
            P(None, "slot", "grp", None, None),
            P(None, ("slot", "grp")),
            P(None, ("slot", "grp")),
            P(None, ("slot", "grp")),
        ),
        check_vma=False,
    )
```

profile of v0, /device:TPU:0, one launch (start us, length us, event | category | flops | bytes accessed | tf_op | source)
XLA Modules:
  0.0 1223.9 jit_solution(11675607025072683181)
XLA Ops:
  0.6 0.8 broadcast_add_fusion
  1.6 3.1 convert_element_type.22
  4.7 7.4 gather_fusion
  12.2 6.1 select_bitcast_fusion.1
  18.8 9.2 reduce.4
  28.0 8.7 reshape.105
  36.7 7.7 all-to-all-start
  45.6 138.7 %all-to-all-done = bf16[32,2,49152]{2,1,0:T(2,128)(2,1)} async-done(((bf16[32,2,49152]{2,1,0:T(2,128)(2,1)}), bf16[32,2,49152]{2,1,0:T(2,128)(2,1)}, u32[]{:S(2)}, u32[]{:S(2)}) %all-to-all-start) | async-done | bytes 6291488 | tf_op jit(solution)/shard_map/all_to_all | solution.py:71
  184.3 21.7 %reshape.106 = bf16[32,1,98304]{2,1,0:T(2,128)(2,1)} reshape(bf16[32,2,49152]{2,1,0:T(2,128)(2,1)} %all-to-all-done) | data formatting | bytes 12582912
  206.0 38.8 %reduce = bf16[32,98304]{1,0:T(8,128)(2,1)} reduce(bf16[32,1,98304]{2,1,0:T(2,128)(2,1)} %reshape.106, bf16[]{:T(256)} %constant.40), dimensions={1}, to_apply=%all_to_all.29.reduce_sub_computation | reduce | bytes 12582914 | tf_op jit(solution)/shard_map/all_to_all | solution.py:71
  244.8 7.2 slice.58
  252.0 7.4 slice.56
  259.4 4.1 fusion.34
  263.6 1.4 convolution_bitcast_fusion.3
  265.0 2.9 multiply_convert_fusion.5
  267.9 2.9 copy.47
  270.8 5.6 convolution_bitcast_fusion.1
  276.4 9.6 copy.37
  286.0 5.6 copy.46
  291.7 9.3 pad_maximum_fusion
  301.0 5.8 all-to-all-start.1
  307.0 275.2 %all-to-all-done.1 = f32[32,1,98304]{2,1,0:T(1,128)} async-done(((f32[32,1,98304]{2,1,0:T(1,128)}), f32[32,1,98304]{2,1,0:T(1,128)}, u32[]{:S(2)}, u32[]{:S(2)}) %all-to-all-start.1) | async-done | bytes 12582944 | tf_op jit(solution)/shard_map/all_to_all | solution.py:81
  582.3 24.2 %fusion.64 = (bf16[16,98304]{1,0:T(8,128)(2,1)S(1)}, f32[16,98304]{1,0:T(8,128)}, f32[16,98304]{1,0:T(8,128)}) fusion(f32[16,98304]{1,0:T(8,128)} %param.17, f32[16,98304]{1,0:T(8,128)} %param.16, f32[16,98304]{1,0:T(8,128)} %param.15, f32[32,1,98304]{2,1,0:T(1,128)} %all-to-all-done.1, s32[32]{0:T(128)S(1)} %reshape.73), kind=kOutput, calls=%fused_computation.88 | convolution fusion | flops 626000384 | bytes 47186048 | tf_op jit(solution)/shard_map/dot_general | solution.py:92
  606.4 7.4 gather_fusion.1
  613.8 6.1 select_bitcast_fusion
  619.9 9.1 reduce.5
  629.0 8.7 reshape.107
  637.8 12.0 all-to-all-start.2
  649.8 0.7 iota_compare_fusion.4
  650.5 139.3 %all-to-all-done.2 = bf16[32,2,49152]{2,1,0:T(2,128)(2,1)} async-done(((bf16[32,2,49152]{2,1,0:T(2,128)(2,1)}), bf16[32,2,49152]{2,1,0:T(2,128)(2,1)}, u32[]{:S(2)}, u32[]{:S(2)}) %all-to-all-start.2) | async-done | bytes 6291488 | tf_op jit(solution)/shard_map/all_to_all | solution.py:71
  789.8 21.7 %reshape.108 = bf16[32,1,98304]{2,1,0:T(2,128)(2,1)} reshape(bf16[32,2,49152]{2,1,0:T(2,128)(2,1)} %all-to-all-done.2) | data formatting | bytes 12582912
  811.4 38.7 %reduce.2 = bf16[32,98304]{1,0:T(8,128)(2,1)} reduce(bf16[32,1,98304]{2,1,0:T(2,128)(2,1)} %reshape.108, bf16[]{:T(256)} %constant.40), dimensions={1}, to_apply=%all_to_all.34.reduce_sub_computation | reduce | bytes 12582914 | tf_op jit(solution)/shard_map/all_to_all | solution.py:71
  850.1 7.3 slice.67
  857.4 7.4 slice.65
  864.8 4.1 fusion.39
  869.0 1.4 convolution_bitcast_fusion.2
  870.4 2.9 multiply_convert_fusion.2
  873.3 2.9 copy.49
  876.2 5.6 convolution_bitcast_fusion
  881.8 9.4 copy.40
  891.2 5.6 copy.48
  896.8 9.3 pad_maximum_fusion.1
  906.1 6.0 all-to-all-start.3
  912.2 4.1 fusion.23
  916.3 4.0 fusion.20
  920.3 1.9 maximum_bitcast_fusion
  922.2 265.3 %all-to-all-done.3 = f32[32,1,98304]{2,1,0:T(1,128)} async-done(((f32[32,1,98304]{2,1,0:T(1,128)}), f32[32,1,98304]{2,1,0:T(1,128)}, u32[]{:S(2)}, u32[]{:S(2)}) %all-to-all-start.3) | async-done | bytes 12582944 | tf_op jit(solution)/shard_map/all_to_all | solution.py:81
  1187.6 36.1 %multiply_subtract_fusion = (f32[16,98304]{1,0:T(8,128)}, f32[16,98304]{1,0:T(8,128)}, f32[16,98304]{1,0:T(8,128)}) fusion(f32[16,98304]{1,0:T(8,128)} %get-tuple-element.25, f32[16,98304]{1,0:T(8,128)} %get-tuple-element.34, f32[16,98304]{1,0:T(8,128)} %param.16, f32[16,98304]{1,0:T(8,128)} %param.15, f32[32,1,98304]{2,1,0:T(1,128)} %all-to-all-done.3, ...), kind=kOutput, calls=%fused_computation.12 | convolution fusion | flops 637010432 | bytes 56623232 | tf_op jit(solution)/shard_map/dot_general | solution.py:92
  (40 shorter events, 2.2 us)
Async XLA Ops:
  36.7 7.7 copy-start.10
  36.7 147.6 %all-to-all-start = ((bf16[32,2,49152]{2,1,0:T(2,128)(2,1)}), bf16[32,2,49152]{2,1,0:T(2,128)(2,1)}, u32[]{:S(2)}, u32[]{:S(2)}) async-start(bf16[32,2,49152]{2,1,0:T(2,128)(2,1)} %reshape.105), calls=%async_computation | async-start | bytes 12582912 | tf_op jit(solution)/shard_map/all_to_all | solution.py:71
  252.0 7.4 copy-start.2
  259.4 4.1 copy-start.11
  267.9 2.9 copy-start.4
  286.0 5.7 copy-start
  301.0 281.3 %all-to-all-start.1 = ((f32[32,1,98304]{2,1,0:T(1,128)}), f32[32,1,98304]{2,1,0:T(1,128)}, u32[]{:S(2)}, u32[]{:S(2)}) async-start(f32[32,1,98304]{2,1,0:T(1,128)} %bitcast.71), calls=%async_computation.1 | async-start | bytes 25165824 | tf_op jit(solution)/shard_map/all_to_all | solution.py:81
  637.8 152.0 %all-to-all-start.2 = ((bf16[32,2,49152]{2,1,0:T(2,128)(2,1)}), bf16[32,2,49152]{2,1,0:T(2,128)(2,1)}, u32[]{:S(2)}, u32[]{:S(2)}) async-start(bf16[32,2,49152]{2,1,0:T(2,128)(2,1)} %reshape.107), calls=%async_computation.2 | async-start | bytes 12582912 | tf_op jit(solution)/shard_map/all_to_all | solution.py:71
  857.4 7.4 copy-start.3
  864.8 4.1 copy-start.12
  873.3 2.9 copy-start.6
  873.3 2.9 copy-start.8
  891.1 5.7 copy-start.1
  906.1 6.0 copy-start.5
  906.1 281.4 %all-to-all-start.3 = ((f32[32,1,98304]{2,1,0:T(1,128)}), f32[32,1,98304]{2,1,0:T(1,128)}, u32[]{:S(2)}, u32[]{:S(2)}) async-start(f32[32,1,98304]{2,1,0:T(1,128)} %bitcast.70), calls=%async_computation.3 | async-start | bytes 25165824 | tf_op jit(solution)/shard_map/all_to_all | solution.py:81
  912.1 4.1 copy-start.7
  912.1 4.1 copy-start.9
where the time goes:
time: 1240 us; the launch traced here: 1220 us
  waiting for transfers between devices  819 us (66%)
  local copies, waits for them, and re-layouts  143 us (12%)
  other arithmetic  134 us (11%)
  matrix products  96.3 us (8%)
  starting transfers between devices  31.5 us (3%)
    all_to_all x2, waiting for transfers between devices, body(): lax.all_to_all(flat_grad.reshape(device_count, shard_len), ('slot', 'grp'...  541 us
    all_to_all x2, waiting for transfers between devices, body(): lax.all_to_all(outgoing, ('slot', 'grp'), split_axis=0, concat_axis=0, ti...  278 us
    all_to_all x6, other arithmetic, body(): lax.all_to_all(outgoing, ('slot', 'grp'), split_axis=0, concat_axis=0, ti...  108 us
    unnamed x34, local copies, waits for them, and re-layouts  77.9 us
    dot_general x2, matrix products, body(): jnp.dot(selector, arrived, precision=lax.Precision.HIGHEST, preferred_ele...  60.3 us
  transfers between devices with their start and end apart: 4, of which 4 were waited for; matrix products, arithmetic and copies ran while one was open for 1% of the time, Pallas kernels for 0%

commit v1 on v0

v1 whole, which is shorter than its diff:
```python
import functools

import jax
import jax.numpy as jnp
from jax import lax
from jax.experimental import pallas as pl
from jax.experimental.pallas import tpu as pltpu
from jax.sharding import PartitionSpec as P

D = 2048
FF = 512
WIDE = 2 * FF
LANES = 128
CHUNKS = 3


beta_one = 0.9
beta_two = 0.99
rho_scale = 2.0
learn_rate = 0.005
grad_scale = 0.25


def silu_parts(values):
    sigmoid = jax.nn.sigmoid(values)
    return (values * sigmoid, sigmoid * (1.0 + values * (1.0 - sigmoid)))


def slot_backward(rows_one, cotangent, live_count, weight_rows):
    w_gateup = weight_rows[:D]
    w_down = weight_rows[D:].reshape(FF, D)
    live = (jnp.arange(rows_one.shape[0], dtype=jnp.int32) < live_count)[:, None]
    masked_ct = jnp.where(live, cotangent, jnp.zeros_like(cotangent))
    preact = jnp.dot(rows_one, w_gateup, preferred_element_type=jnp.float32)
    gate_pre = preact[:, :FF]
    up_pre = preact[:, FF:]
    activated, slope = silu_parts(gate_pre)
    hidden = (activated * up_pre).astype(jnp.bfloat16)
    hidden_grad = lax.dot_general(
        masked_ct, w_down, (((1,), (1,)), ((), ())), preferred_element_type=jnp.float32
    )
    pre_grad = jnp.concatenate(
        [hidden_grad * up_pre * slope, hidden_grad * activated], axis=1
    ).astype(jnp.bfloat16)
    grad_gateup = lax.dot_general(
        rows_one, pre_grad, (((0,), (0,)), ((), ())), preferred_element_type=jnp.float32
    ).astype(jnp.bfloat16)
    grad_down = lax.dot_general(
        hidden, masked_ct, (((0,), (0,)), ((), ())), preferred_element_type=jnp.float32
    ).astype(jnp.bfloat16)
    row_grad = lax.dot_general(
        pre_grad, w_gateup, (((1,), (1,)), ((), ())), preferred_element_type=jnp.float32
    ).astype(jnp.bfloat16)
    return row_grad, jnp.concatenate([grad_gateup, grad_down.reshape(-1, WIDE)])


def pack_out(experts, rows, ids_ref, staged, out_ref):
    span = experts * rows

    def one(dest, carry):
        base = ids_ref[dest] * rows
        for lane in range(WIDE // LANES):
            piece = staged[pl.ds(pl.multiple_of(lane * span + base, 8), rows), :]
            out_ref[dest, :, lane * LANES:(lane + 1) * LANES] = piece.astype(jnp.bfloat16)
        return carry

    lax.fori_loop(0, out_ref.shape[0], one, 0)


def pack_kernel(experts, rows, ids_ref, w_ref, out_ref, staged):
    span = experts * rows
    for row in range(rows):
        for lane in range(WIDE // LANES):
            at = row * WIDE + lane * LANES
            staged[pl.ds(lane * span + row, experts, stride=rows), :] = w_ref[:, at:at + LANES]
    pack_out(experts, rows, ids_ref, staged, out_ref)


def sophia_kernel(experts, rows, packs, kept, *refs):
    ids_ref, next_ref, got_ref, m_ref, c_ref, w_ref = refs[:6]
    refs = refs[6 + kept:]
    m_out, c_out, w_out = refs[:3]
    total = refs[-1]
    span = experts * rows
    total[...] = jnp.zeros_like(total)

    def add(source, carry):
        base = ids_ref[source] * rows
        for lane in range(WIDE // LANES):
            at = pl.ds(pl.multiple_of(lane * span + base, 8), rows)
            piece = got_ref[source, :, lane * LANES:(lane + 1) * LANES]
            total[at, :] = total[at, :] + piece.astype(jnp.float32)
        return carry

    lax.fori_loop(0, got_ref.shape[0], add, 0)
    for row in range(rows):
        for lane in range(WIDE // LANES):
            at = pl.ds(lane * span + row, experts, stride=rows)
            cols = pl.ds(row * WIDE + lane * LANES, LANES)
            grads = total[at, :] * grad_scale
            moment = beta_one * m_ref[:, cols] + (1.0 - beta_one) * grads
            curve = beta_two * c_ref[:, cols] + (1.0 - beta_two) * grads * grads
            weight = w_ref[:, cols] - learn_rate * jnp.clip(
                moment / (rho_scale * curve), -1.0, 1.0
            )
            m_out[:, cols] = moment
            c_out[:, cols] = curve
            w_out[:, cols] = weight
            if packs:
                total[at, :] = weight
    if packs:
        pack_out(experts, rows, next_ref, total, refs[3])


def block_rows(chunk_rows):
    return 16 if chunk_rows % 16 == 0 else chunk_rows


def pack_chunk(chunk, chunk_rows, ids, master):
    experts, devices = master.shape[0], ids.shape[0]
    rows = block_rows(chunk_rows)
    steps = chunk_rows // rows
    return pl.pallas_call(
        functools.partial(pack_kernel, experts, rows),
        grid_spec=pltpu.PrefetchScalarGridSpec(
            num_scalar_prefetch=1,
            grid=(steps,),
            in_specs=[pl.BlockSpec((experts, rows * WIDE), lambda i, *_: (0, chunk * steps + i))],
            out_specs=pl.BlockSpec((devices, rows, WIDE), lambda i, *_: (0, i, 0)),
            scratch_shapes=[pltpu.VMEM((WIDE // LANES * experts * rows, LANES), jnp.float32)],
        ),
        out_shape=jax.ShapeDtypeStruct((devices, chunk_rows, WIDE), jnp.bfloat16),
        name="pack",
    )(ids, master)


def sophia_chunk(chunk, chunk_rows, ids, next_ids, got, state, whole, final):
    experts, devices = state[0].shape[0], ids.shape[0]
    rows = block_rows(chunk_rows)
    steps = chunk_rows // rows
    shift = chunk * steps
    kept = 0 if whole is None else 3
    near = pl.BlockSpec((experts, rows * WIDE), lambda i, *_: (0, i))
    far = pl.BlockSpec((experts, rows * WIDE), lambda i, *_: (0, shift + i))
    packed = pl.BlockSpec((devices, rows, WIDE), lambda i, *_: (0, i, 0))
    width = chunk_rows * WIDE * (CHUNKS if final else 1)
    out_shape = [jax.ShapeDtypeStruct((experts, width), jnp.float32)] * 3
    out_specs = [far if final else near] * 3
    if not final:
        out_shape = out_shape + [jax.ShapeDtypeStruct((devices, chunk_rows, WIDE), jnp.bfloat16)]
        out_specs = out_specs + [packed]
    return pl.pallas_call(
        functools.partial(sophia_kernel, experts, rows, not final, kept),
        grid_spec=pltpu.PrefetchScalarGridSpec(
            num_scalar_prefetch=2,
            grid=(steps,),
            in_specs=[packed]
            + [near if final else far] * 3
            + [pl.BlockSpec(memory_space=pl.ANY)] * kept,
            out_specs=out_specs,
            scratch_shapes=[pltpu.VMEM((WIDE // LANES * experts * rows, LANES), jnp.float32)],
        ),
        out_shape=out_shape,
        input_output_aliases={6 + i: i for i in range(kept)},
        name="sophia",
    )(ids, next_ids, got, *state, *(whole or ()))


def body(token_rows, cotangents, row_counts, old_place, new_place, momentum, curvature, master):
    group_count = lax.axis_size("grp")
    slot_count = lax.axis_size("slot")
    device_count = group_count * slot_count
    experts = master.shape[0]
    per_group = experts // group_count
    chunk_rows = master.shape[1] // (CHUNKS * WIDE)
    owners = (jnp.arange(group_count, dtype=jnp.int32) * per_group)[None, :]
    ids = [(place + owners).reshape(-1) for place in (old_place, new_place)]

    def swap(array):
        return lax.all_to_all(array, ("slot", "grp"), split_axis=0, concat_axis=0, tiled=True)

    arrived = [swap(pack_chunk(k, chunk_rows, ids[0], master)) for k in range(CHUNKS)]
    outputs = []
    states = [(momentum, curvature, master)] * CHUNKS
    whole = None
    for step_index in range(2):
        final = step_index == 1
        weight_rows = jnp.stack(arrived, axis=1).reshape(-1, WIDE)
        row_grad, grad_rows = slot_backward(
            token_rows[step_index, 0, 0],
            cotangents[step_index, 0, 0],
            row_counts[step_index, 0, 0],
            weight_rows,
        )
        outputs.append(row_grad)
        grad_rows = grad_rows.reshape(device_count, CHUNKS, chunk_rows, WIDE)
        got = [swap(grad_rows[:, k]) for k in range(CHUNKS)]
        arrived = []
        for k in range(CHUNKS):
            result = sophia_chunk(
                k, chunk_rows, ids[step_index], ids[1], got[k], states[k], whole, final
            )
            if final:
                whole = tuple(result)
            else:
                states[k] = tuple(result[:3])
                arrived.append(swap(result[3]))
    return (jnp.stack(outputs)[:, None, None], *whole)


def solution(mesh):
    return jax.shard_map(
        body,
        mesh=mesh,
        in_specs=(
            P(None, "slot", "grp", None, None),
            P(None, "slot", "grp", None, None),
            P(None, "slot", "grp"),
            P(),
            P(),
            P(None, ("slot", "grp")),
            P(None, ("slot", "grp")),
            P(None, ("slot", "grp")),
        ),
        out_specs=(
            P(None, "slot", "grp", None, None),
            P(None, ("slot", "grp")),
            P(None, ("slot", "grp")),
            P(None, ("slot", "grp")),
        ),
        check_vma=False,
    )
```

time: 1240 us -> 746 us (0.60); the launches traced: 1220 us -> 744 us
  waiting for transfers between devices: 819 us -> 330 us
  blocking collectives: 0 us -> 210 us
  other arithmetic: 134 us -> 16.9 us
  local copies, waits for them, and re-layouts: 143 us -> 63.2 us
  matrix products: 96.3 us -> 27.6 us
  Pallas kernels: 0 us -> 60.6 us
    all_to_all x4 -> x8, waiting for transfers between devices: 819 us -> 330 us  [swap(): lax.all_to_all(array, ('slot', 'grp'), split_axis=0, concat_axis=0, tiled...]
    all_to_all x0 -> x4, blocking collectives: none -> 210 us  [swap(): lax.all_to_all(array, ('slot', 'grp'), split_axis=0, concat_axis=0, tiled...]
    all_to_all x6 -> x0, other arithmetic: 108 us -> none  [body(): lax.all_to_all(outgoing, ('slot', 'grp'), split_axis=0, concat_axis=0, ti...]
    unnamed x34 -> x36, local copies, waits for them, and re-layouts: 77.9 us -> 9.66 us
    pallas_call x0 -> x9, Pallas kernels: none -> 60.6 us  [the longest x6 46.4 us: sophia_chunk(): pl.pallas_call(functools.partial(sophia_kernel, experts, rows, not final,...]
    dot_general x2 -> x0, matrix products: 60.3 us -> none  [body(): jnp.dot(selector, arrived, precision=lax.Precision.HIGHEST, preferred_ele...]
    slice x4 -> x2, local copies, waits for them, and re-layouts: 29.3 us -> 0.34 us  [slot_backward(): w_down = weight_rows[D:].reshape(FF, D)]
    reshape x2 -> x8, local copies, waits for them, and re-layouts: 0.16 us -> 21.5 us  [the longest x4 16 us: slot_backward(): grad_down.reshape(-1, WIDE)]
  transfers between devices with their start and end apart: 4 -> 8, of which waited for: 4 -> 8; matrix products, arithmetic and copies ran while one was open for 1% -> 1% of each run, Pallas kernels for 0% -> 7%
where the time goes in v1:
time: 746 us; the launch traced here: 744 us
  waiting for transfers between devices  330 us (44%)
  blocking collectives  210 us (28%)
  local copies, waits for them, and re-layouts  63.2 us (8%)
  Pallas kernels  60.6 us (8%)
  starting transfers between devices  35.8 us (5%)
  matrix products  27.6 us (4%)
  other arithmetic  16.9 us (2%)
    all_to_all x8, waiting for transfers between devices, swap(): lax.all_to_all(array, ('slot', 'grp'), split_axis=0, concat_axis=0, tiled...  330 us
    all_to_all x4, blocking collectives, swap(): lax.all_to_all(array, ('slot', 'grp'), split_axis=0, concat_axis=0, tiled...  210 us
    pallas_call x6, Pallas kernels, sophia_chunk(): pl.pallas_call(functools.partial(sophia_kernel, experts, rows, not final,...  46.4 us
    all_to_all x8, starting transfers between devices, swap(): lax.all_to_all(array, ('slot', 'grp'), split_axis=0, concat_axis=0, tiled...  35.8 us
    concatenate x2, local copies, waits for them, and re-layouts, slot_backward(): jnp.concatenate([grad_gateup, grad_down.reshape(-1, WIDE)])  17.2 us
    reshape x4, local copies, waits for them, and re-layouts, slot_backward(): grad_down.reshape(-1, WIDE)  16 us
  transfers between devices with their start and end apart: 8, of which 8 were waited for; matrix products, arithmetic and copies ran while one was open for 1% of the time, Pallas kernels for 7%

profile of v1, /device:TPU:0, one launch (start us, length us, event | category | flops | bytes accessed | tf_op | source)
XLA Modules:
  0.0 744.3 jit_solution(11433971269185806321)
XLA Ops:
  2.1 4.7 pack.5
  6.8 7.3 all-to-all-start.2
  14.2 4.7 pack.4
  18.9 44.0 %all-to-all-done.2 = bf16[32,32,1024]{2,1,0:T(8,128)(2,1)S(1)} async-done(((bf16[32,32,1024]{2,1,0:T(8,128)(2,1)}), bf16[32,32,1024]{2,1,0:T(8,128)(2,1)S(1)}, u32[]{:S(2)}, u32[]{:S(2)}) %all-to-all-start.2) | async-done | bytes 2097184 | tf_op jit(solution)/shard_map/all_to_all | solution.py:180
  62.9 4.1 all-to-all-start.1
  67.0 4.7 pack.3
  71.8 43.9 %all-to-all-done.1 = bf16[32,32,1024]{2,1,0:T(8,128)(2,1)} async-done(((bf16[32,32,1024]{2,1,0:T(8,128)(2,1)}), bf16[32,32,1024]{2,1,0:T(8,128)(2,1)}, u32[]{:S(2)}, u32[]{:S(2)}) %all-to-all-start.1) | async-done | bytes 2097184 | tf_op jit(solution)/shard_map/all_to_all | solution.py:180
  115.7 4.1 all-to-all-start
  121.2 47.4 %all-to-all-done = bf16[32,32,1024]{2,1,0:T(8,128)(2,1)} async-done(((bf16[32,32,1024]{2,1,0:T(8,128)(2,1)}), bf16[32,32,1024]{2,1,0:T(8,128)(2,1)}, u32[]{:S(2)}, u32[]{:S(2)}) %all-to-all-start) | async-done | bytes 2097184 | tf_op jit(solution)/shard_map/all_to_all | solution.py:180
  168.6 3.2 pad_maximum_fusion
  173.3 4.0 copy-done.8
  180.3 2.7 convolution_convert_fusion.1
  183.0 4.1 reshape.70
  187.0 3.9 copy.27
  193.1 3.9 multiply_convert_fusion.5
  199.4 3.3 pad_maximum_fusion.1
  202.7 8.6 %copy.28 = bf16[3072,1024]{1,0:T(8,128)(2,1)} copy(bf16[3072,1024]{0,1:T(8,128)(2,1)} %pad_maximum_fusion.1) | data formatting | bytes 12582912 | tf_op jit(solution)/shard_map/concatenate | solution.py:54
  211.3 5.5 slice_bitcast_fusion.5
  216.8 52.6 %all_to_all.60.refs_2_ = bf16[32,32,1024]{2,1,0:T(8,128)(2,1)} all-to-all(bf16[32,32,1024]{2,1,0:T(8,128)(2,1)S(1)} %get-tuple-element.57), channel_id=1, replica_groups=mesh['slot'=8,'grp'=4] {'slot','grp'}, dimensions={0} | all-to-all | bytes 4194304 | tf_op jit(solution)/shard_map/all_to_all | solution.py:180
  269.4 52.2 %all_to_all.61.refs_2_ = bf16[32,32,1024]{2,1,0:T(8,128)(2,1)} all-to-all(bf16[32,32,1024]{2,1,0:T(8,128)(2,1)S(1)} %get-tuple-element.59), channel_id=1, replica_groups=mesh['slot'=8,'grp'=4] {'slot','grp'}, dimensions={0} | all-to-all | bytes 4194304 | tf_op jit(solution)/shard_map/all_to_all | solution.py:180
  321.6 3.8 all-to-all-start.5
  326.2 8.5 %sophia.8 = (f32[16,32768]{1,0:T(8,128)}, f32[16,32768]{1,0:T(8,128)}, f32[16,32768]{1,0:T(8,128)}, bf16[32,32,1024]{2,1,0:T(8,128)(2,1)}) custom-call(s32[32]{0:T(128)} %reshape.66.ids_ref.refs_0_, s32[32]{0:T(128)} %reshape.69.refs_1_.refs_0_, bf16[32,32,1024]{2,1,0:T(8,128)(2,1)} %all_to_all.61.refs_2_, f32[16,98304]{1,0:T(8,128)} %refs_3_.5, ...), custom_call_target="tpu_custom_call" | custom-call | tf_op jit(solution)/shard_map/sophia/pallas_call | solution.py:152
  334.7 39.3 %all-to-all-done.5.refs_2_ = bf16[32,32,1024]{2,1,0:T(8,128)(2,1)S(1)} async-done(((bf16[32,32,1024]{2,1,0:T(8,128)(2,1)}), bf16[32,32,1024]{2,1,0:T(8,128)(2,1)S(1)}, u32[]{:S(2)}, u32[]{:S(2)}) %all-to-all-start.5) | async-done | bytes 2097184 | tf_op jit(solution)/shard_map/all_to_all | solution.py:180
  375.3 4.0 all-to-all-start.8
  379.4 8.5 %sophia.7 = (f32[16,32768]{1,0:T(8,128)}, f32[16,32768]{1,0:T(8,128)}, f32[16,32768]{1,0:T(8,128)}, bf16[32,32,1024]{2,1,0:T(8,128)(2,1)}) custom-call(s32[32]{0:T(128)} %reshape.66.ids_ref.refs_0_, s32[32]{0:T(128)} %reshape.69.refs_1_.refs_0_, bf16[32,32,1024]{2,1,0:T(8,128)(2,1)} %copy-done.4, f32[16,98304]{1,0:T(8,128)} %refs_3_.5, f32[16,98304]{1,0:T(8,128)} %refs_4_.5, ...), custom_call_target="tpu_custom_call" | custom-call | tf_op jit(solution)/shard_map/sophia/pallas_call | solution.py:152
  387.9 40.2 %all-to-all-done.8 = bf16[32,32,1024]{2,1,0:T(8,128)(2,1)S(1)} async-done(((bf16[32,32,1024]{2,1,0:T(8,128)(2,1)}), bf16[32,32,1024]{2,1,0:T(8,128)(2,1)S(1)}, u32[]{:S(2)}, u32[]{:S(2)}) %all-to-all-start.8) | async-done | bytes 2097184 | tf_op jit(solution)/shard_map/all_to_all | solution.py:180
  428.1 4.1 all-to-all-start.6
  432.2 8.5 %sophia.6 = (f32[16,32768]{1,0:T(8,128)}, f32[16,32768]{1,0:T(8,128)}, f32[16,32768]{1,0:T(8,128)}, bf16[32,32,1024]{2,1,0:T(8,128)(2,1)}) custom-call(s32[32]{0:T(128)} %reshape.66.ids_ref.refs_0_, s32[32]{0:T(128)} %reshape.69.refs_1_.refs_0_, bf16[32,32,1024]{2,1,0:T(8,128)(2,1)} %all_to_all.60.refs_2_, f32[16,98304]{1,0:T(8,128)} %refs_3_.5, ...), custom_call_target="tpu_custom_call" | custom-call | tf_op jit(solution)/shard_map/sophia/pallas_call | solution.py:152
  440.7 40.2 %all-to-all-done.6 = bf16[32,32,1024]{2,1,0:T(8,128)(2,1)} async-done(((bf16[32,32,1024]{2,1,0:T(8,128)(2,1)}), bf16[32,32,1024]{2,1,0:T(8,128)(2,1)}, u32[]{:S(2)}, u32[]{:S(2)}) %all-to-all-start.6) | async-done | bytes 2097184 | tf_op jit(solution)/shard_map/all_to_all | solution.py:180
  480.9 4.1 all-to-all-start.4
  485.7 48.1 %all-to-all-done.4 = bf16[32,32,1024]{2,1,0:T(8,128)(2,1)} async-done(((bf16[32,32,1024]{2,1,0:T(8,128)(2,1)}), bf16[32,32,1024]{2,1,0:T(8,128)(2,1)}, u32[]{:S(2)}, u32[]{:S(2)}) %all-to-all-start.4) | async-done | bytes 2097184 | tf_op jit(solution)/shard_map/all_to_all | solution.py:180
  533.8 3.2 pad_maximum_fusion.2
  543.5 2.7 convolution_convert_fusion
  546.2 4.1 reshape.74
  550.2 3.9 copy.34
  556.3 3.9 multiply_convert_fusion.2
  560.2 2.4 convert_bitcast_fusion
  562.6 3.3 pad_maximum_fusion.3
  565.9 8.6 %copy.35 = bf16[3072,1024]{1,0:T(8,128)(2,1)} copy(bf16[3072,1024]{0,1:T(8,128)(2,1)} %pad_maximum_fusion.3) | data formatting | bytes 12582912 | tf_op jit(solution)/shard_map/concatenate | solution.py:54
  574.5 5.5 slice_bitcast_fusion
  580.0 52.6 %all_to_all.62.refs_2_ = bf16[32,32,1024]{2,1,0:T(8,128)(2,1)} all-to-all(bf16[32,32,1024]{2,1,0:T(8,128)(2,1)S(1)} %get-tuple-element.54), channel_id=1, replica_groups=mesh['slot'=8,'grp'=4] {'slot','grp'}, dimensions={0} | all-to-all | bytes 4194304 | tf_op jit(solution)/shard_map/all_to_all | solution.py:180
  632.6 52.2 %all_to_all.63.refs_2_ = bf16[32,32,1024]{2,1,0:T(8,128)(2,1)} all-to-all(bf16[32,32,1024]{2,1,0:T(8,128)(2,1)S(1)} %get-tuple-element.55), channel_id=1, replica_groups=mesh['slot'=8,'grp'=4] {'slot','grp'}, dimensions={0} | all-to-all | bytes 4194304 | tf_op jit(solution)/shard_map/all_to_all | solution.py:180
  684.9 4.0 all-to-all-start.9
  688.9 4.2 fusion.17
  696.9 6.9 sophia.9
  703.9 7.0 sophia.10
  710.8 26.5 %all-to-all-done.9.refs_2_ = bf16[32,32,1024]{2,1,0:T(8,128)(2,1)} async-done(((bf16[32,32,1024]{2,1,0:T(8,128)(2,1)}), bf16[32,32,1024]{2,1,0:T(8,128)(2,1)}, u32[]{:S(2)}, u32[]{:S(2)}) %all-to-all-start.9) | async-done | bytes 2097184 | tf_op jit(solution)/shard_map/all_to_all | solution.py:180
  737.4 7.0 sophia.11
  (56 shorter events, 26.8 us)
Async XLA Ops:
  6.8 56.0 %all-to-all-start.2 = ((bf16[32,32,1024]{2,1,0:T(8,128)(2,1)}), bf16[32,32,1024]{2,1,0:T(8,128)(2,1)S(1)}, u32[]{:S(2)}, u32[]{:S(2)}) async-start(bf16[32,32,1024]{2,1,0:T(8,128)(2,1)} %pack.5), calls=%async_computation.2 | async-start | bytes 4194304 | tf_op jit(solution)/shard_map/all_to_all | solution.py:180
  62.9 52.8 %all-to-all-start.1 = ((bf16[32,32,1024]{2,1,0:T(8,128)(2,1)}), bf16[32,32,1024]{2,1,0:T(8,128)(2,1)}, u32[]{:S(2)}, u32[]{:S(2)}) async-start(bf16[32,32,1024]{2,1,0:T(8,128)(2,1)} %pack.4), calls=%async_computation.1 | async-start | bytes 4194304 | tf_op jit(solution)/shard_map/all_to_all | solution.py:180
  71.8 48.1 %copy-start.5 = (s32[2,1,1]{0,2,1:T(1,128)S(1)}, s32[2,1,1]{0,2,1:T(1,128)}, u32[]{:S(2)}) copy-start(s32[2,1,1]{0,2,1:T(1,128)} %param.10) | copy-start | bytes 28
  115.7 52.8 %all-to-all-start = ((bf16[32,32,1024]{2,1,0:T(8,128)(2,1)}), bf16[32,32,1024]{2,1,0:T(8,128)(2,1)}, u32[]{:S(2)}, u32[]{:S(2)}) async-start(bf16[32,32,1024]{2,1,0:T(8,128)(2,1)} %pack.3), calls=%async_computation | async-start | bytes 4194304 | tf_op jit(solution)/shard_map/all_to_all | solution.py:180
  173.1 6.0 copy-start
  173.1 4.2 copy-start.8
  177.3 3.0 copy-start.6
  179.1 1.1 copy-start.13
  193.1 3.9 copy-start.9
  197.0 2.4 copy-start.2
  321.6 52.4 %all-to-all-start.5 = ((bf16[32,32,1024]{2,1,0:T(8,128)(2,1)}), bf16[32,32,1024]{2,1,0:T(8,128)(2,1)S(1)}, u32[]{:S(2)}, u32[]{:S(2)}) async-start(bf16[32,32,1024]{2,1,0:T(8,128)(2,1)} %get-tuple-element.58), calls=%async_computation.5 | async-start | bytes 4194304 | tf_op jit(solution)/shard_map/all_to_all | solution.py:180
  374.0 1.3 copy-start.4
  375.3 52.7 %all-to-all-start.8 = ((bf16[32,32,1024]{2,1,0:T(8,128)(2,1)}), bf16[32,32,1024]{2,1,0:T(8,128)(2,1)S(1)}, u32[]{:S(2)}, u32[]{:S(2)}) async-start(bf16[32,32,1024]{2,1,0:T(8,128)(2,1)} %get-tuple-element.27), calls=%async_computation.8 | async-start | bytes 4194304 | tf_op jit(solution)/shard_map/all_to_all | solution.py:180
  428.1 52.8 %all-to-all-start.6 = ((bf16[32,32,1024]{2,1,0:T(8,128)(2,1)}), bf16[32,32,1024]{2,1,0:T(8,128)(2,1)}, u32[]{:S(2)}, u32[]{:S(2)}) async-start(bf16[32,32,1024]{2,1,0:T(8,128)(2,1)} %get-tuple-element.26), calls=%async_computation.6 | async-start | bytes 4194304 | tf_op jit(solution)/shard_map/all_to_all | solution.py:180
  480.9 52.8 %all-to-all-start.4 = ((bf16[32,32,1024]{2,1,0:T(8,128)(2,1)}), bf16[32,32,1024]{2,1,0:T(8,128)(2,1)}, u32[]{:S(2)}, u32[]{:S(2)}) async-start(bf16[32,32,1024]{2,1,0:T(8,128)(2,1)} %get-tuple-element.25), calls=%async_computation.4 | async-start | bytes 4194304 | tf_op jit(solution)/shard_map/all_to_all | solution.py:180
  537.0 1.9 copy-start.10
  538.3 2.7 copy-start.1
  541.0 1.2 copy-start.12
  541.0 2.5 copy-start.7
  556.3 3.9 copy-start.11
  560.2 2.4 copy-start.14
  560.2 2.4 copy-start.3
  684.9 8.2 %slice-start = ((s8[6291456]{0:T(1024)(128)(4,1)}), s8[2097152]{0:T(1024)(128)(4,1)S(1)}, s32[]{:S(2)}) async-start(s8[6291456]{0:T(1024)(128)(4,1)} %bitcast.91), calls=%async_computation.12 | async-start | bytes 4194304
  684.9 52.5 %all-to-all-start.9 = ((bf16[32,32,1024]{2,1,0:T(8,128)(2,1)}), bf16[32,32,1024]{2,1,0:T(8,128)(2,1)}, u32[]{:S(2)}, u32[]{:S(2)}) async-start(bf16[32,32,1024]{2,1,0:T(8,128)(2,1)} %get-tuple-element.56), calls=%async_computation.9 | async-start | bytes 4194304 | tf_op jit(solution)/shard_map/all_to_all | solution.py:180
  688.9 4.2 slice-start.1
  688.9 4.2 copy-start.15

commit v2 on v1

--- a/solution.py
+++ b/solution.py
@@ -11,7 +11,10 @@
 FF = 512
 WIDE = 2 * FF
 LANES = 128
+TILE = 256
 CHUNKS = 3
+FIRST = ((0, 1), (1, 2))
+REST = ((0, 2), (2, 1))
 
 
 beta_one = 0.9
@@ -26,32 +29,159 @@
     return (values * sigmoid, sigmoid * (1.0 + values * (1.0 - sigmoid)))
 
 
-def slot_backward(rows_one, cotangent, live_count, weight_rows):
-    w_gateup = weight_rows[:D]
-    w_down = weight_rows[D:].reshape(FF, D)
-    live = (jnp.arange(rows_one.shape[0], dtype=jnp.int32) < live_count)[:, None]
-    masked_ct = jnp.where(live, cotangent, jnp.zeros_like(cotangent))
-    preact = jnp.dot(rows_one, w_gateup, preferred_element_type=jnp.float32)
-    gate_pre = preact[:, :FF]
-    up_pre = preact[:, FF:]
-    activated, slope = silu_parts(gate_pre)
-    hidden = (activated * up_pre).astype(jnp.bfloat16)
-    hidden_grad = lax.dot_general(
-        masked_ct, w_down, (((1,), (1,)), ((), ())), preferred_element_type=jnp.float32
-    )
-    pre_grad = jnp.concatenate(
-        [hidden_grad * up_pre * slope, hidden_grad * activated], axis=1
-    ).astype(jnp.bfloat16)
-    grad_gateup = lax.dot_general(
-        rows_one, pre_grad, (((0,), (0,)), ((), ())), preferred_element_type=jnp.float32
-    ).astype(jnp.bfloat16)
-    grad_down = lax.dot_general(
-        hidden, masked_ct, (((0,), (0,)), ((), ())), preferred_element_type=jnp.float32
-    ).astype(jnp.bfloat16)
-    row_grad = lax.dot_general(
-        pre_grad, w_gateup, (((1,), (1,)), ((), ())), preferred_element_type=jnp.float32
-    ).astype(jnp.bfloat16)
-    return row_grad, jnp.concatenate([grad_gateup, grad_down.reshape(-1, WIDE)])
+def contract(left, right, dims):
+    return lax.dot_general(left, right, ((dims[:1], dims[1:]), ((), ())), preferred_element_type=jnp.float32)
+
+
+def move_rows(spans, unit, chunk_refs, whole, sem, inward):
+    share = whole.shape[0] // chunk_refs[0].shape[0]
+    for (start, count), ref in zip(spans, chunk_refs):
+        rows = count * unit
+
+        def one(device, carry):
+            part = whole.at[pl.ds(pl.multiple_of(device * share + start * unit, 8), rows), :]
+            ends = (ref.at[device], part) if inward else (part, ref.at[device])
+            pltpu.make_async_copy(*ends, sem).start()
+            return carry
+
+        lax.fori_loop(0, ref.shape[0], one, 0)
+
+
+def spread(half):
+    row = lax.broadcasted_iota(jnp.int32, (TILE // 2, TILE), 0)
+    column = lax.broadcasted_iota(jnp.int32, (TILE // 2, TILE), 1)
+    return jnp.where(column == 2 * row + half, 1.0, 0.0).astype(jnp.bfloat16)
+
+
+def tiles(extent, size, step):
+    def one(index, carry):
+        step(pl.ds(pl.multiple_of(index * size, size), size), index)
+        return carry
+
+    lax.fori_loop(0, extent // size, one, 0)
+
+
+def slot_kernel(spans_in, spans_out, unit, count_ref, x_ref, ct_ref, *refs):
+    n_in, n_out = len(spans_in), len(spans_out)
+    arrived, refs = refs[:n_in], refs[n_in:]
+    grads_out, refs = refs[:n_out], refs[n_out:]
+    dz, weights, grads, masked, preact, halves, hidden, hidden_up, sem = refs
+    move_rows(spans_in, unit, arrived, weights, sem.at[0], True)
+    live_count = count_ref[0]
+
+    def mask(at, index):
+        values = ct_ref[at, :].astype(jnp.float32)
+        row = index * 16 + lax.broadcasted_iota(jnp.int32, values.shape, 0)
+        masked[at, :] = jnp.where(row < live_count, values, 0.0).astype(jnp.bfloat16)
+
+    tiles(ct_ref.shape[0], 16, mask)
+    pltpu.make_async_copy(weights, weights, sem.at[0]).wait()
+
+    def forward(at, index):
+        preact[:, at] = contract(x_ref[...], weights[:D, at], (1, 0))
+
+    tiles(WIDE, TILE, forward)
+
+    def split(at, index):
+        part = weights[pl.ds(pl.multiple_of(D + index * TILE, TILE), TILE), :]
+        to = pl.ds(pl.multiple_of(index * (TILE // 2), TILE // 2), TILE // 2)
+        for half in range(2):
+            halves[half, to, :] = contract(spread(half), part, (1, 0)).astype(jnp.bfloat16)
+
+    tiles(WIDE, TILE, split)
+
+    def backward(at, index):
+        hidden_grad = contract(masked[:, :WIDE], halves[0, at, :], (1, 1))
+        hidden_grad = hidden_grad + contract(masked[:, WIDE:], halves[1, at, :], (1, 1))
+        up_at = pl.ds(pl.multiple_of(FF + index * TILE, TILE), TILE)
+        up_pre = preact[:, up_at]
+        activated, slope = silu_parts(preact[:, at])
+        hidden[:, at] = (activated * up_pre).astype(jnp.bfloat16)
+        dz[:, at] = (hidden_grad * up_pre * slope).astype(jnp.bfloat16)
+        dz[:, up_at] = (hidden_grad * activated).astype(jnp.bfloat16)
+
+    tiles(FF, TILE, backward)
+
+    def widen(at, index):
+        part = hidden[:, pl.ds(pl.multiple_of(index * (TILE // 2), TILE // 2), TILE // 2)]
+        for half in range(2):
+            hidden_up[half, :, at] = contract(part, spread(half), (1, 0)).astype(jnp.bfloat16)
+
+    tiles(WIDE, TILE, widen)
+
+    def gateup(at, index):
+        grads[at, :] = contract(x_ref[:, at], dz[...], (0, 0)).astype(jnp.bfloat16)
+
+    tiles(D, TILE, gateup)
+
+    def down(at, index):
+        total = contract(hidden_up[0, :, at], masked[:, :WIDE], (0, 0))
+        total = total + contract(hidden_up[1, :, at], masked[:, WIDE:], (0, 0))
+        to = pl.ds(pl.multiple_of(D + index * TILE, TILE), TILE)
+        grads[to, :] = total.astype(jnp.bfloat16)
+
+    tiles(WIDE, TILE, down)
+    move_rows(spans_out, unit, grads_out, grads, sem.at[1], False)
+    pltpu.make_async_copy(grads, grads, sem.at[1]).wait()
+
+
+def rows_kernel(spans_in, unit, kept, dz_ref, *refs):
+    arrived = refs[:len(spans_in)]
+    out_ref, weights, sem = refs[len(spans_in) + kept:]
+    move_rows(spans_in, unit, arrived, weights, sem.at[0], True)
+    pltpu.make_async_copy(weights, weights, sem.at[0]).wait()
+
+    def one(at, index):
+        out_ref[:, at] = contract(dz_ref[...], weights[at, :], (1, 1)).astype(jnp.bfloat16)
+
+    tiles(D, TILE, one)
+
+
+def slot_backward(step, spans_in, spans_out, unit, token_rows, cotangents, live_count, arrived):
+    devices, cap = arrived[0].shape[0], token_rows.shape[3]
+    rows = devices * CHUNKS * unit
+    mine = pl.BlockSpec((None, None, None, cap, D), lambda i: (step, 0, 0, 0, 0))
+    any_spec = pl.BlockSpec(memory_space=pl.ANY)
+    out = pl.pallas_call(
+        functools.partial(slot_kernel, spans_in, spans_out, unit),
+        grid=(1,),
+        in_specs=[pl.BlockSpec(memory_space=pltpu.SMEM), mine, mine] + [any_spec] * len(arrived),
+        out_specs=[any_spec] * len(spans_out) + [pl.BlockSpec((cap, WIDE), lambda i: (0, 0))],
+        out_shape=[
+            jax.ShapeDtypeStruct((devices, count * unit, WIDE), jnp.bfloat16)
+            for _, count in spans_out
+        ]
+        + [jax.ShapeDtypeStruct((cap, WIDE), jnp.bfloat16)],
+        scratch_shapes=[
+            pltpu.VMEM((rows, WIDE), jnp.bfloat16),
+            pltpu.VMEM((rows, WIDE), jnp.bfloat16),
+            pltpu.VMEM((cap, D), jnp.bfloat16),
+            pltpu.VMEM((cap, WIDE), jnp.float32),
+            pltpu.VMEM((2, FF, WIDE), jnp.bfloat16),
+            pltpu.VMEM((cap, FF), jnp.bfloat16),
+            pltpu.VMEM((2, cap, WIDE), jnp.bfloat16),
+            pltpu.SemaphoreType.DMA((2,)),
+        ],
+        name="slot",
+    )(live_count, token_rows, cotangents, *arrived)
+    return out[:-1], out[-1]
+
+
+def row_grads(step, spans_in, unit, pre_grad, arrived, shape, before):
+    devices, cap = arrived[0].shape[0], pre_grad.shape[0]
+    rows = devices * CHUNKS * unit
+    kept = [] if before is None else [before]
+    any_spec = pl.BlockSpec(memory_space=pl.ANY)
+    return pl.pallas_call(
+        functools.partial(rows_kernel, spans_in, unit, len(kept)),
+        grid=(1,),
+        in_specs=[pl.BlockSpec((cap, WIDE), lambda i: (0, 0))] + [any_spec] * (len(arrived) + len(kept)),
+        out_specs=pl.BlockSpec((None, None, None, cap, D), lambda i: (step, 0, 0, 0, 0)),
+        out_shape=jax.ShapeDtypeStruct(shape, jnp.bfloat16),
+        scratch_shapes=[pltpu.VMEM((rows, WIDE), jnp.bfloat16), pltpu.SemaphoreType.DMA((1,))],
+        input_output_aliases={1 + len(arrived): 0} if kept else {},
+        name="rows",
+    )(pre_grad, *arrived, *kept)
 
 
 def pack_out(experts, rows, ids_ref, staged, out_ref):
@@ -116,16 +246,18 @@
     return 16 if chunk_rows % 16 == 0 else chunk_rows
 
 
-def pack_chunk(chunk, chunk_rows, ids, master):
+def pack_chunk(span, unit, ids, master):
     experts, devices = master.shape[0], ids.shape[0]
-    rows = block_rows(chunk_rows)
+    rows = block_rows(unit)
+    chunk_rows = span[1] * unit
     steps = chunk_rows // rows
+    shift = span[0] * unit // rows
     return pl.pallas_call(
         functools.partial(pack_kernel, experts, rows),
         grid_spec=pltpu.PrefetchScalarGridSpec(
             num_scalar_prefetch=1,
             grid=(steps,),
-            in_specs=[pl.BlockSpec((experts, rows * WIDE), lambda i, *_: (0, chunk * steps + i))],
+            in_specs=[pl.BlockSpec((experts, rows * WIDE), lambda i, *_: (0, shift + i))],
             out_specs=pl.BlockSpec((devices, rows, WIDE), lambda i, *_: (0, i, 0)),
             scratch_shapes=[pltpu.VMEM((WIDE // LANES * experts * rows, LANES), jnp.float32)],
         ),
@@ -134,16 +266,17 @@
     )(ids, master)
 
 
-def sophia_chunk(chunk, chunk_rows, ids, next_ids, got, state, whole, final):
+def sophia_chunk(span, unit, ids, next_ids, got, state, whole, final):
     experts, devices = state[0].shape[0], ids.shape[0]
-    rows = block_rows(chunk_rows)
+    rows = block_rows(unit)
+    chunk_rows = span[1] * unit
     steps = chunk_rows // rows
-    shift = chunk * steps
+    shift = span[0] * unit // rows
     kept = 0 if whole is None else 3
     near = pl.BlockSpec((experts, rows * WIDE), lambda i, *_: (0, i))
     far = pl.BlockSpec((experts, rows * WIDE), lambda i, *_: (0, shift + i))
     packed = pl.BlockSpec((devices, rows, WIDE), lambda i, *_: (0, i, 0))
-    width = chunk_rows * WIDE * (CHUNKS if final else 1)
+    width = unit * CHUNKS * WIDE if final else chunk_rows * WIDE
     out_shape = [jax.ShapeDtypeStruct((experts, width), jnp.float32)] * 3
     out_specs = [far if final else near] * 3
     if not final:
@@ -172,40 +305,36 @@
     device_count = group_count * slot_count
     experts = master.shape[0]
     per_group = experts // group_count
-    chunk_rows = master.shape[1] // (CHUNKS * WIDE)
+    unit = master.shape[1] // (CHUNKS * WIDE)
     owners = (jnp.arange(group_count, dtype=jnp.int32) * per_group)[None, :]
     ids = [(place + owners).reshape(-1) for place in (old_place, new_place)]
 
     def swap(array):
         return lax.all_to_all(array, ("slot", "grp"), split_axis=0, concat_axis=0, tiled=True)
 
-    arrived = [swap(pack_chunk(k, chunk_rows, ids[0], master)) for k in range(CHUNKS)]
-    outputs = []
-    states = [(momentum, curvature, master)] * CHUNKS
+    spans = FIRST
+    arrived = [swap(pack_chunk(span, unit, ids[0], master)) for span in spans]
+    rows_out = None
+    states = [(momentum, curvature, master)] * len(REST)
     whole = None
-    for step_index in range(2):
-        final = step_index == 1
-        weight_rows = jnp.stack(arrived, axis=1).reshape(-1, WIDE)
-        row_grad, grad_rows = slot_backward(
-            token_rows[step_index, 0, 0],
-            cotangents[step_index, 0, 0],
-            row_counts[step_index, 0, 0],
-            weight_rows,
+    for step in range(2):
+        final = step == 1
+        grads, pre_grad = slot_backward(
+            step, spans, REST, unit, token_rows, cotangents, row_counts[step, 0], arrived
         )
-        outputs.append(row_grad)
-        grad_rows = grad_rows.reshape(device_count, CHUNKS, chunk_rows, WIDE)
-        got = [swap(grad_rows[:, k]) for k in range(CHUNKS)]
-        arrived = []
-        for k in range(CHUNKS):
-            result = sophia_chunk(
-                k, chunk_rows, ids[step_index], ids[1], got[k], states[k], whole, final
-            )
+        got = [swap(part) for part in grads]
+        rows_out = row_grads(
+            step, spans, unit, pre_grad, arrived, token_rows.shape, rows_out
+        )
+        spans, arrived = REST, []
+        for k, span in enumerate(REST):
+            result = sophia_chunk(span, unit, ids[step], ids[1], got[k], states[k], whole, final)
             if final:
                 whole = tuple(result)
             else:
                 states[k] = tuple(result[:3])
                 arrived.append(swap(result[3]))
-    return (jnp.stack(outputs)[:, None, None], *whole)
+    return (rows_out, *whole)
 
 
 def solution(mesh):

time: 746 us -> 667 us (0.89)
  local copies, waits for them, and re-layouts: 63.2 us -> 3.43 us
  waiting for transfers between devices: 330 us -> 273 us
  Pallas kernels: 60.6 us -> 115 us
  blocking collectives: 210 us -> 249 us
  matrix products: 27.6 us -> 0 us
  other arithmetic: 16.9 us -> 0.77 us
  starting transfers between devices: 35.8 us -> 24.2 us
    pallas_call x0 -> x4, Pallas kernels: none -> 60.1 us  [the longest x2 43.3 us: slot_backward(): pl.pallas_call(functools.partial(slot_kernel, spans_in, spans_out, unit),...]
    all_to_all x8 -> x5, waiting for transfers between devices: 330 us -> 273 us  [swap(): lax.all_to_all(array, ('slot', 'grp'), split_axis=0, concat_axis=0, tiled...]
    all_to_all x4 -> x3, blocking collectives: 210 us -> 249 us  [swap(): lax.all_to_all(array, ('slot', 'grp'), split_axis=0, concat_axis=0, tiled...]
    dot_general x10 -> x0, matrix products: 27.6 us -> none  [the longest x2 7.76 us: slot_backward(): lax.dot_general(masked_ct, w_down, (((1,), (1,)), ((), ())), preferred_el...]
    reshape x6 -> x0, local copies, waits for them, and re-layouts: 20.2 us -> none  [the longest x4 16 us: slot_backward(): grad_down.reshape(-1, WIDE)]
    concatenate x2 -> x0, local copies, waits for them, and re-layouts: 17.2 us -> none  [slot_backward(): jnp.concatenate([grad_gateup, grad_down.reshape(-1, WIDE)])]
    all_to_all x8 -> x5, starting transfers between devices: 35.8 us -> 24.2 us  [swap(): lax.all_to_all(array, ('slot', 'grp'), split_axis=0, concat_axis=0, tiled...]
    squeeze x2 -> x0, local copies, waits for them, and re-layouts: 11 us -> none  [body(): got = [swap(grad_rows[:, k]) for k in range(CHUNKS)]]
  transfers between devices with their start and end apart: 8 -> 5, of which waited for: 8 -> 5; matrix products, arithmetic and copies ran while one was open for 1% -> 0% of each run, Pallas kernels for 7% -> 9%
where the time goes in v2:
time: 667 us; the launch traced here: 666 us
  waiting for transfers between devices  273 us (41%)
  blocking collectives  249 us (37%)
  Pallas kernels  115 us (17%)
  starting transfers between devices  24.2 us (4%)
    all_to_all x5, waiting for transfers between devices, swap(): lax.all_to_all(array, ('slot', 'grp'), split_axis=0, concat_axis=0, tiled...  273 us
    all_to_all x3, blocking collectives, swap(): lax.all_to_all(array, ('slot', 'grp'), split_axis=0, concat_axis=0, tiled...  249 us
    pallas_call x4, Pallas kernels, sophia_chunk(): pl.pallas_call(functools.partial(sophia_kernel, experts, rows, not final,...  43.3 us
    pallas_call x2, Pallas kernels, slot_backward(): pl.pallas_call(functools.partial(slot_kernel, spans_in, spans_out, unit),...  43.3 us
    all_to_all x5, starting transfers between devices, swap(): lax.all_to_all(array, ('slot', 'grp'), split_axis=0, concat_axis=0, tiled...  24.2 us
    pallas_call x2, Pallas kernels, row_grads(): pl.pallas_call(functools.partial(rows_kernel, spans_in, unit, len(kept)),...  16.8 us
  transfers between devices with their start and end apart: 5, of which 5 were waited for; matrix products, arithmetic and copies ran while one was open for 0% of the time, Pallas kernels for 9%

profile of v2, /device:TPU:0, one launch (start us, length us, event | category | flops | bytes accessed | tf_op | source)
XLA Modules:
  0.0 666.1 jit_solution(7372449778976915018)
XLA Ops:
  0.6 0.8 broadcast_add_fusion
  1.4 0.1 copy.18
  1.5 0.6 reshape.18.ids_ref.refs_0_
  2.1 4.7 pack.2
  6.8 7.3 %all-to-all-start = ((bf16[32,32,1024]{2,1,0:T(8,128)(2,1)}), bf16[32,32,1024]{2,1,0:T(8,128)(2,1)S(1)}, u32[]{:S(2)}, u32[]{:S(2)}) async-start(bf16[32,32,1024]{2,1,0:T(8,128)(2,1)} %pack.2), calls=%async_computation | async-start | bytes 4194304 | tf_op jit(solution)/shard_map/all_to_all | solution.py:313
  14.2 7.4 %pack.3 = bf16[32,64,1024]{2,1,0:T(8,128)(2,1)} custom-call(s32[32]{0:T(128)} %reshape.18.ids_ref.refs_0_, f32[16,98304]{1,0:T(8,128)} %refs_5_.3), custom_call_target="tpu_custom_call" | custom-call | tf_op jit(solution)/shard_map/pack/pallas_call | solution.py:255
  21.5 0.0 copy-start.3
  21.5 41.4 %all-to-all-done.refs_0_ = bf16[32,32,1024]{2,1,0:T(8,128)(2,1)S(1)} async-done(((bf16[32,32,1024]{2,1,0:T(8,128)(2,1)}), bf16[32,32,1024]{2,1,0:T(8,128)(2,1)S(1)}, u32[]{:S(2)}, u32[]{:S(2)}) %all-to-all-start) | async-done | bytes 2097184 | tf_op jit(solution)/shard_map/all_to_all | solution.py:313
  62.9 0.0 copy-start
  62.9 4.1 all-to-all-start.1
  67.0 0.0 copy-done.3
  67.1 0.6 fusion
  67.7 0.0 copy-done
  67.7 93.6 %all-to-all-done.1.refs_1_ = bf16[32,64,1024]{2,1,0:T(8,128)(2,1)} async-done(((bf16[32,64,1024]{2,1,0:T(8,128)(2,1)}), bf16[32,64,1024]{2,1,0:T(8,128)(2,1)}, u32[]{:S(2)}, u32[]{:S(2)}) %all-to-all-start.1) | async-done | bytes 4194336 | tf_op jit(solution)/shard_map/all_to_all | solution.py:313
  161.3 21.7 %slot.2 = (bf16[32,64,1024]{2,1,0:T(8,128)(2,1)}, bf16[32,32,1024]{2,1,0:T(8,128)(2,1)}, bf16[384,1024]{1,0:T(8,128)(2,1)}) custom-call(s32[1]{0:T(128)} %bitcast.1.count_ref, bf16[2,1,1,384,2048]{4,3,2,1,0:T(8,128)(2,1)} %x_ref.3, bf16[2,1,1,384,2048]{4,3,2,1,0:T(8,128)(2,1)} %ct_ref.3, bf16[32,32,1024]{2,1,0:T(8,128)(2,1)} %copy-done, ...), custom_call_target="tpu_custom_call" | custom-call | tf_op jit(solution)/shard_map/slot/pallas_call | solution.py:145
  183.0 53.9 %all_to_all.40.refs_2_ = bf16[32,32,1024]{2,1,0:T(8,128)(2,1)} all-to-all(bf16[32,32,1024]{2,1,0:T(8,128)(2,1)} %get-tuple-element.26), channel_id=1, replica_groups=mesh['slot'=8,'grp'=4] {'slot','grp'}, dimensions={0} | all-to-all | bytes 4194304 | tf_op jit(solution)/shard_map/all_to_all | solution.py:313
  236.8 3.8 all-to-all-start.2
  240.6 0.1 copy.19
  240.7 0.7 reshape.19.refs_1_.refs_0_
  241.4 8.5 %sophia.5 = (f32[16,32768]{1,0:T(8,128)}, f32[16,32768]{1,0:T(8,128)}, f32[16,32768]{1,0:T(8,128)}, bf16[32,32,1024]{2,1,0:T(8,128)(2,1)}) custom-call(s32[32]{0:T(128)} %reshape.18.ids_ref.refs_0_, s32[32]{0:T(128)} %reshape.19.refs_1_.refs_0_, bf16[32,32,1024]{2,1,0:T(8,128)(2,1)} %all_to_all.40.refs_2_, f32[16,98304]{1,0:T(8,128)} %refs_3_.3, ...), custom_call_target="tpu_custom_call" | custom-call | tf_op jit(solution)/shard_map/sophia/pallas_call | solution.py:285
  249.9 85.0 %all-to-all-done.2.refs_2_ = bf16[32,64,1024]{2,1,0:T(8,128)(2,1)} async-done(((bf16[32,64,1024]{2,1,0:T(8,128)(2,1)}), bf16[32,64,1024]{2,1,0:T(8,128)(2,1)}, u32[]{:S(2)}, u32[]{:S(2)}) %all-to-all-start.2) | async-done | bytes 4194336 | tf_op jit(solution)/shard_map/all_to_all | solution.py:313
  334.9 5.1 all-to-all-start.5
  339.9 15.4 %sophia.4 = (f32[16,65536]{1,0:T(8,128)}, f32[16,65536]{1,0:T(8,128)}, f32[16,65536]{1,0:T(8,128)}, bf16[32,64,1024]{2,1,0:T(8,128)(2,1)}) custom-call(s32[32]{0:T(128)} %reshape.18.ids_ref.refs_0_, s32[32]{0:T(128)} %reshape.19.refs_1_.refs_0_, bf16[32,64,1024]{2,1,0:T(8,128)(2,1)} %all-to-all-done.2.refs_2_, f32[16,98304]{1,0:T(8,128)} %refs_3_.3, ...), custom_call_target="tpu_custom_call" | custom-call | tf_op jit(solution)/shard_map/sophia/pallas_call | solution.py:285
  355.4 33.3 %all-to-all-done.5.refs_1_ = bf16[32,32,1024]{2,1,0:T(8,128)(2,1)S(1)} async-done(((bf16[32,32,1024]{2,1,0:T(8,128)(2,1)}), bf16[32,32,1024]{2,1,0:T(8,128)(2,1)S(1)}, u32[]{:S(2)}, u32[]{:S(2)}) %all-to-all-start.5) | async-done | bytes 2097184 | tf_op jit(solution)/shard_map/all_to_all | solution.py:313
  388.6 0.0 copy-start.1
  388.6 97.7 %all_to_all.41.refs_0_ = bf16[32,64,1024]{2,1,0:T(8,128)(2,1)} all-to-all(bf16[32,64,1024]{2,1,0:T(8,128)(2,1)} %get-tuple-element.25), channel_id=1, replica_groups=mesh['slot'=8,'grp'=4] {'slot','grp'}, dimensions={0} | all-to-all | bytes 8388608 | tf_op jit(solution)/shard_map/all_to_all | solution.py:313
  486.4 0.0 copy-done.1
  486.4 21.6 %slot.3 = (bf16[32,64,1024]{2,1,0:T(8,128)(2,1)}, bf16[32,32,1024]{2,1,0:T(8,128)(2,1)}, bf16[384,1024]{1,0:T(8,128)(2,1)}) custom-call(s32[1]{0:T(128)} %bitcast.count_ref, bf16[2,1,1,384,2048]{4,3,2,1,0:T(8,128)(2,1)} %x_ref.3, bf16[2,1,1,384,2048]{4,3,2,1,0:T(8,128)(2,1)} %ct_ref.3, bf16[32,64,1024]{2,1,0:T(8,128)(2,1)} %all_to_all.41.refs_0_, ...), custom_call_target="tpu_custom_call" | custom-call | tf_op jit(solution)/shard_map/slot/pallas_call | solution.py:145
  508.0 97.4 %all_to_all.42.refs_2_ = bf16[32,64,1024]{2,1,0:T(8,128)(2,1)} all-to-all(bf16[32,64,1024]{2,1,0:T(8,128)(2,1)} %get-tuple-element.34), channel_id=1, replica_groups=mesh['slot'=8,'grp'=4] {'slot','grp'}, dimensions={0} | all-to-all | bytes 8388608 | tf_op jit(solution)/shard_map/all_to_all | solution.py:313
  605.4 3.8 all-to-all-start.6
  609.2 8.4 %rows.2.refs_2_ = bf16[2,1,1,384,2048]{4,3,2,1,0:T(8,128)(2,1)} custom-call(bf16[384,1024]{1,0:T(8,128)(2,1)} %get-tuple-element.29.dz_ref, bf16[32,32,1024]{2,1,0:T(8,128)(2,1)} %copy-done, bf16[32,64,1024]{2,1,0:T(8,128)(2,1)} %all-to-all-done.1.refs_1_), custom_call_target="tpu_custom_call" | custom-call | tf_op jit(solution)/shard_map/rows/pallas_call | solution.py:175
  617.7 8.4 %rows.3 = bf16[2,1,1,384,2048]{4,3,2,1,0:T(8,128)(2,1)} custom-call(bf16[384,1024]{1,0:T(8,128)(2,1)} %get-tuple-element.28.dz_ref, bf16[32,64,1024]{2,1,0:T(8,128)(2,1)} %all_to_all.41.refs_0_, bf16[32,32,1024]{2,1,0:T(8,128)(2,1)} %copy-done.1, bf16[2,1,1,384,2048]{4,3,2,1,0:T(8,128)(2,1)} %rows.2.refs_2_), custom_call_target="tpu_custom_call", output_to_operand_aliasing={{}: (3, {})} | custom-call | tf_op jit(solution)/shard_map/rows/pallas_call | solution.py:175
  626.0 12.4 %sophia.6 = (f32[16,98304]{1,0:T(8,128)}, f32[16,98304]{1,0:T(8,128)}, f32[16,98304]{1,0:T(8,128)}) custom-call(s32[32]{0:T(128)} %reshape.19.refs_1_.refs_0_, s32[32]{0:T(128)} %reshape.19.refs_1_.refs_0_, bf16[32,64,1024]{2,1,0:T(8,128)(2,1)} %all_to_all.42.refs_2_, f32[16,65536]{1,0:T(8,128)} %get-tuple-element.35.refs_3_, ...), custom_call_target="tpu_custom_call" | custom-call | tf_op jit(solution)/shard_map/sophia/pallas_call | solution.py:285
  638.4 19.3 %all-to-all-done.6.refs_2_ = bf16[32,32,1024]{2,1,0:T(8,128)(2,1)S(1)} async-done(((bf16[32,32,1024]{2,1,0:T(8,128)(2,1)}), bf16[32,32,1024]{2,1,0:T(8,128)(2,1)S(1)}, u32[]{:S(2)}, u32[]{:S(2)}) %all-to-all-start.6) | async-done | bytes 2097184 | tf_op jit(solution)/shard_map/all_to_all | solution.py:313
  657.8 0.0 copy-start.2
  657.8 1.3 copy-done.2
  659.1 7.0 %sophia.7 = (f32[16,98304]{1,0:T(8,128)}, f32[16,98304]{1,0:T(8,128)}, f32[16,98304]{1,0:T(8,128)}) custom-call(s32[32]{0:T(128)} %reshape.19.refs_1_.refs_0_, s32[32]{0:T(128)} %reshape.19.refs_1_.refs_0_, bf16[32,32,1024]{2,1,0:T(8,128)(2,1)} %copy-done.2, ...), custom_call_target="tpu_custom_call", output_to_operand_aliasing={{0}: (6, {}), {1}: (7, {}), {2}: (8, {})} | custom-call | tf_op jit(solution)/shard_map/sophia/pallas_call | solution.py:285
  (1 shorter events, 0.0 us)
Async XLA Ops:
  6.8 56.0 %all-to-all-start = ((bf16[32,32,1024]{2,1,0:T(8,128)(2,1)}), bf16[32,32,1024]{2,1,0:T(8,128)(2,1)S(1)}, u32[]{:S(2)}, u32[]{:S(2)}) async-start(bf16[32,32,1024]{2,1,0:T(8,128)(2,1)} %pack.2), calls=%async_computation | async-start | bytes 4194304 | tf_op jit(solution)/shard_map/all_to_all | solution.py:313
  21.5 45.5 %copy-start.3 = (s32[2,1,1]{0,2,1:T(1,128)S(1)}, s32[2,1,1]{0,2,1:T(1,128)}, u32[]{:S(2)}) copy-start(s32[2,1,1]{0,2,1:T(1,128)} %param.10) | copy-start | bytes 28
  62.9 4.8 copy-start
  62.9 98.4 %all-to-all-start.1 = ((bf16[32,64,1024]{2,1,0:T(8,128)(2,1)}), bf16[32,64,1024]{2,1,0:T(8,128)(2,1)}, u32[]{:S(2)}, u32[]{:S(2)}) async-start(bf16[32,64,1024]{2,1,0:T(8,128)(2,1)} %pack.3), calls=%async_computation.1 | async-start | bytes 8388608 | tf_op jit(solution)/shard_map/all_to_all | solution.py:313
  236.8 98.0 %all-to-all-start.2 = ((bf16[32,64,1024]{2,1,0:T(8,128)(2,1)}), bf16[32,64,1024]{2,1,0:T(8,128)(2,1)}, u32[]{:S(2)}, u32[]{:S(2)}) async-start(bf16[32,64,1024]{2,1,0:T(8,128)(2,1)} %get-tuple-element.24), calls=%async_computation.2 | async-start | bytes 8388608 | tf_op jit(solution)/shard_map/all_to_all | solution.py:313
  334.9 53.8 %all-to-all-start.5 = ((bf16[32,32,1024]{2,1,0:T(8,128)(2,1)}), bf16[32,32,1024]{2,1,0:T(8,128)(2,1)S(1)}, u32[]{:S(2)}, u32[]{:S(2)}) async-start(bf16[32,32,1024]{2,1,0:T(8,128)(2,1)} %get-tuple-element.27), calls=%async_computation.5 | async-start | bytes 4194304 | tf_op jit(solution)/shard_map/all_to_all | solution.py:313
  388.6 97.8 %copy-start.1 = (bf16[32,32,1024]{2,1,0:T(8,128)(2,1)}, bf16[32,32,1024]{2,1,0:T(8,128)(2,1)S(1)}, u32[]{:S(2)}) copy-start(bf16[32,32,1024]{2,1,0:T(8,128)(2,1)S(1)} %all-to-all-done.5.refs_1_) | copy-start | bytes 6291460
  605.4 52.4 %all-to-all-start.6 = ((bf16[32,32,1024]{2,1,0:T(8,128)(2,1)}), bf16[32,32,1024]{2,1,0:T(8,128)(2,1)S(1)}, u32[]{:S(2)}, u32[]{:S(2)}) async-start(bf16[32,32,1024]{2,1,0:T(8,128)(2,1)} %get-tuple-element.30), calls=%async_computation.6 | async-start | bytes 4194304 | tf_op jit(solution)/shard_map/all_to_all | solution.py:313
  657.8 1.3 copy-start.2

commit v3 on v2

--- a/solution.py
+++ b/solution.py
@@ -33,7 +33,7 @@
     return lax.dot_general(left, right, ((dims[:1], dims[1:]), ((), ())), preferred_element_type=jnp.float32)
 
 
-def move_rows(spans, unit, chunk_refs, whole, sem, inward):
+def move_rows(spans, unit, chunk_refs, whole, sem, inward, low, high):
     share = whole.shape[0] // chunk_refs[0].shape[0]
     for (start, count), ref in zip(spans, chunk_refs):
         rows = count * unit
@@ -44,7 +44,12 @@
             pltpu.make_async_copy(*ends, sem).start()
             return carry
 
-        lax.fori_loop(0, ref.shape[0], one, 0)
+        lax.fori_loop(low, high, one, 0)
+
+
+def await_rows(whole, low, high, sem):
+    part = whole.at[low:high, :]
+    pltpu.make_async_copy(part, part, sem).wait()
 
 
 def spread(half):
@@ -61,26 +66,37 @@
     lax.fori_loop(0, extent // size, one, 0)
 
 
-def slot_kernel(spans_in, spans_out, unit, count_ref, x_ref, ct_ref, *refs):
+def slot_kernel(step, spans_in, spans_out, unit, count_ref, x_in, ct_in, *refs):
     n_in, n_out = len(spans_in), len(spans_out)
     arrived, refs = refs[:n_in], refs[n_in:]
     grads_out, refs = refs[:n_out], refs[n_out:]
-    dz, weights, grads, masked, preact, halves, hidden, hidden_up, sem = refs
-    move_rows(spans_in, unit, arrived, weights, sem.at[0], True)
+    dz, weights, grads, x_ref, masked, preact, halves, hidden, hidden_up, sem = refs
+    devices = arrived[0].shape[0]
+    share = weights.shape[0] // devices
+    early = pl.cdiv(D, share)
+    ct_copy = pltpu.make_async_copy(ct_in.at[step, 0, 0], masked, sem.at[2])
+    x_copy = pltpu.make_async_copy(x_in.at[step, 0, 0], x_ref, sem.at[3])
+    ct_copy.start()
+    x_copy.start()
+    move_rows(spans_in, unit, arrived, weights, sem.at[0], True, 0, early)
+    move_rows(spans_in, unit, arrived, weights, sem.at[4], True, early, devices)
     live_count = count_ref[0]
+    ct_copy.wait()
 
     def mask(at, index):
-        values = ct_ref[at, :].astype(jnp.float32)
+        values = masked[at, :].astype(jnp.float32)
         row = index * 16 + lax.broadcasted_iota(jnp.int32, values.shape, 0)
         masked[at, :] = jnp.where(row < live_count, values, 0.0).astype(jnp.bfloat16)
 
-    tiles(ct_ref.shape[0], 16, mask)
-    pltpu.make_async_copy(weights, weights, sem.at[0]).wait()
+    tiles(masked.shape[0], 16, mask)
+    x_copy.wait()
+    await_rows(weights, 0, early * share, sem.at[0])
 
     def forward(at, index):
         preact[:, at] = contract(x_ref[...], weights[:D, at], (1, 0))
 
     tiles(WIDE, TILE, forward)
+    await_rows(weights, early * share, devices * share, sem.at[4])
 
     def split(at, index):
         part = weights[pl.ds(pl.multiple_of(D + index * TILE, TILE), TILE), :]
@@ -109,8 +125,13 @@
 
     tiles(WIDE, TILE, widen)
 
+    def send(index):
+        low, high = index * TILE // share, (index + 1) * TILE // share
+        move_rows(spans_out, unit, grads_out, grads, sem.at[1], False, low, high)
+
     def gateup(at, index):
         grads[at, :] = contract(x_ref[:, at], dz[...], (0, 0)).astype(jnp.bfloat16)
+        send(index)
 
     tiles(D, TILE, gateup)
 
@@ -119,17 +140,19 @@
         total = total + contract(hidden_up[1, :, at], masked[:, WIDE:], (0, 0))
         to = pl.ds(pl.multiple_of(D + index * TILE, TILE), TILE)
         grads[to, :] = total.astype(jnp.bfloat16)
+        send(D // TILE + index)
 
     tiles(WIDE, TILE, down)
-    move_rows(spans_out, unit, grads_out, grads, sem.at[1], False)
     pltpu.make_async_copy(grads, grads, sem.at[1]).wait()
 
 
 def rows_kernel(spans_in, unit, kept, dz_ref, *refs):
     arrived = refs[:len(spans_in)]
     out_ref, weights, sem = refs[len(spans_in) + kept:]
-    move_rows(spans_in, unit, arrived, weights, sem.at[0], True)
-    pltpu.make_async_copy(weights, weights, sem.at[0]).wait()
+    early = pl.cdiv(D, weights.shape[0] // arrived[0].shape[0])
+    share = weights.shape[0] // arrived[0].shape[0]
+    move_rows(spans_in, unit, arrived, weights, sem.at[0], True, 0, early)
+    await_rows(weights, 0, early * share, sem.at[0])
 
     def one(at, index):
         out_ref[:, at] = contract(dz_ref[...], weights[at, :], (1, 1)).astype(jnp.bfloat16)
@@ -140,12 +163,11 @@
 def slot_backward(step, spans_in, spans_out, unit, token_rows, cotangents, live_count, arrived):
     devices, cap = arrived[0].shape[0], token_rows.shape[3]
     rows = devices * CHUNKS * unit
-    mine = pl.BlockSpec((None, None, None, cap, D), lambda i: (step, 0, 0, 0, 0))
     any_spec = pl.BlockSpec(memory_space=pl.ANY)
     out = pl.pallas_call(
-        functools.partial(slot_kernel, spans_in, spans_out, unit),
+        functools.partial(slot_kernel, step, spans_in, spans_out, unit),
         grid=(1,),
-        in_specs=[pl.BlockSpec(memory_space=pltpu.SMEM), mine, mine] + [any_spec] * len(arrived),
+        in_specs=[pl.BlockSpec(memory_space=pltpu.SMEM)] + [any_spec] * (2 + len(arrived)),
         out_specs=[any_spec] * len(spans_out) + [pl.BlockSpec((cap, WIDE), lambda i: (0, 0))],
         out_shape=[
             jax.ShapeDtypeStruct((devices, count * unit, WIDE), jnp.bfloat16)
@@ -156,11 +178,12 @@
             pltpu.VMEM((rows, WIDE), jnp.bfloat16),
             pltpu.VMEM((rows, WIDE), jnp.bfloat16),
             pltpu.VMEM((cap, D), jnp.bfloat16),
+            pltpu.VMEM((cap, D), jnp.bfloat16),
             pltpu.VMEM((cap, WIDE), jnp.float32),
             pltpu.VMEM((2, FF, WIDE), jnp.bfloat16),
             pltpu.VMEM((cap, FF), jnp.bfloat16),
             pltpu.VMEM((2, cap, WIDE), jnp.bfloat16),
-            pltpu.SemaphoreType.DMA((2,)),
+            pltpu.SemaphoreType.DMA((5,)),
         ],
         name="slot",
     )(live_count, token_rows, cotangents, *arrived)

time: 667 us -> 661 us (level)
  Pallas kernels: 115 us -> 108 us
where the time goes in v3:
time: 661 us; the launch traced here: 660 us
  waiting for transfers between devices  274 us (41%)
  blocking collectives  249 us (38%)
  Pallas kernels  108 us (16%)
  starting transfers between devices  24.2 us (4%)
    all_to_all x5, waiting for transfers between devices, swap(): lax.all_to_all(array, ('slot', 'grp'), split_axis=0, concat_axis=0, tiled...  274 us
    all_to_all x3, blocking collectives, swap(): lax.all_to_all(array, ('slot', 'grp'), split_axis=0, concat_axis=0, tiled...  249 us
    pallas_call x4, Pallas kernels, sophia_chunk(): pl.pallas_call(functools.partial(sophia_kernel, experts, rows, not final,...  43.3 us
    pallas_call x2, Pallas kernels, slot_backward(): pl.pallas_call(functools.partial(slot_kernel, step, spans_in, spans_out,...  37 us
    all_to_all x5, starting transfers between devices, swap(): lax.all_to_all(array, ('slot', 'grp'), split_axis=0, concat_axis=0, tiled...  24.2 us
    pallas_call x2, Pallas kernels, row_grads(): pl.pallas_call(functools.partial(rows_kernel, spans_in, unit, len(kept)),...  15.6 us
  transfers between devices with their start and end apart: 5, of which 5 were waited for; matrix products, arithmetic and copies ran while one was open for 0% of the time, Pallas kernels for 9%

profile of v3, /device:TPU:0, one launch (start us, length us, event | category | flops | bytes accessed | tf_op | source)
XLA Modules:
  0.0 659.8 jit_solution(3677359074581219984)
XLA Ops:
  0.6 0.8 broadcast_add_fusion
  1.4 0.1 copy.18
  1.5 0.6 reshape.18.ids_ref.refs_0_
  2.1 4.7 pack.2
  6.8 7.3 %all-to-all-start = ((bf16[32,32,1024]{2,1,0:T(8,128)(2,1)}), bf16[32,32,1024]{2,1,0:T(8,128)(2,1)S(1)}, u32[]{:S(2)}, u32[]{:S(2)}) async-start(bf16[32,32,1024]{2,1,0:T(8,128)(2,1)} %pack.2), calls=%async_computation | async-start | bytes 4194304 | tf_op jit(solution)/shard_map/all_to_all | solution.py:336
  14.2 7.4 %pack.3 = bf16[32,64,1024]{2,1,0:T(8,128)(2,1)} custom-call(s32[32]{0:T(128)} %reshape.18.ids_ref.refs_0_, f32[16,98304]{1,0:T(8,128)} %refs_5_.3), custom_call_target="tpu_custom_call" | custom-call | tf_op jit(solution)/shard_map/pack/pallas_call | solution.py:278
  21.5 0.0 copy-start.3
  21.5 41.4 %all-to-all-done.refs_0_ = bf16[32,32,1024]{2,1,0:T(8,128)(2,1)S(1)} async-done(((bf16[32,32,1024]{2,1,0:T(8,128)(2,1)}), bf16[32,32,1024]{2,1,0:T(8,128)(2,1)S(1)}, u32[]{:S(2)}, u32[]{:S(2)}) %all-to-all-start) | async-done | bytes 2097184 | tf_op jit(solution)/shard_map/all_to_all | solution.py:336
  62.9 0.0 copy-start
  62.9 4.1 all-to-all-start.1
  67.0 0.0 copy-done.3
  67.1 0.6 fusion
  67.7 0.0 copy-done
  67.7 93.6 %all-to-all-done.1.refs_1_ = bf16[32,64,1024]{2,1,0:T(8,128)(2,1)} async-done(((bf16[32,64,1024]{2,1,0:T(8,128)(2,1)}), bf16[32,64,1024]{2,1,0:T(8,128)(2,1)}, u32[]{:S(2)}, u32[]{:S(2)}) %all-to-all-start.1) | async-done | bytes 4194336 | tf_op jit(solution)/shard_map/all_to_all | solution.py:336
  161.3 18.5 %slot.2 = (bf16[32,64,1024]{2,1,0:T(8,128)(2,1)}, bf16[32,32,1024]{2,1,0:T(8,128)(2,1)}, bf16[384,1024]{1,0:T(8,128)(2,1)}) custom-call(s32[1]{0:T(128)} %bitcast.1.count_ref, bf16[2,1,1,384,2048]{4,3,2,1,0:T(8,128)(2,1)} %x_in.3, bf16[2,1,1,384,2048]{4,3,2,1,0:T(8,128)(2,1)} %ct_in.3, bf16[32,32,1024]{2,1,0:T(8,128)(2,1)} %copy-done, ...), custom_call_target="tpu_custom_call" | custom-call | tf_op jit(solution)/shard_map/slot/pallas_call | solution.py:167
  179.8 53.8 %all_to_all.40.refs_2_ = bf16[32,32,1024]{2,1,0:T(8,128)(2,1)} all-to-all(bf16[32,32,1024]{2,1,0:T(8,128)(2,1)} %get-tuple-element.26), channel_id=1, replica_groups=mesh['slot'=8,'grp'=4] {'slot','grp'}, dimensions={0} | all-to-all | bytes 4194304 | tf_op jit(solution)/shard_map/all_to_all | solution.py:336
  233.7 3.8 all-to-all-start.2
  237.5 0.1 copy.19
  237.6 0.7 reshape.19.refs_1_.refs_0_
  238.2 8.5 %sophia.5 = (f32[16,32768]{1,0:T(8,128)}, f32[16,32768]{1,0:T(8,128)}, f32[16,32768]{1,0:T(8,128)}, bf16[32,32,1024]{2,1,0:T(8,128)(2,1)}) custom-call(s32[32]{0:T(128)} %reshape.18.ids_ref.refs_0_, s32[32]{0:T(128)} %reshape.19.refs_1_.refs_0_, bf16[32,32,1024]{2,1,0:T(8,128)(2,1)} %all_to_all.40.refs_2_, f32[16,98304]{1,0:T(8,128)} %refs_3_.3, ...), custom_call_target="tpu_custom_call" | custom-call | tf_op jit(solution)/shard_map/sophia/pallas_call | solution.py:308
  246.7 85.0 %all-to-all-done.2.refs_2_ = bf16[32,64,1024]{2,1,0:T(8,128)(2,1)} async-done(((bf16[32,64,1024]{2,1,0:T(8,128)(2,1)}), bf16[32,64,1024]{2,1,0:T(8,128)(2,1)}, u32[]{:S(2)}, u32[]{:S(2)}) %all-to-all-start.2) | async-done | bytes 4194336 | tf_op jit(solution)/shard_map/all_to_all | solution.py:336
  331.7 5.1 all-to-all-start.5
  336.8 15.4 %sophia.4 = (f32[16,65536]{1,0:T(8,128)}, f32[16,65536]{1,0:T(8,128)}, f32[16,65536]{1,0:T(8,128)}, bf16[32,64,1024]{2,1,0:T(8,128)(2,1)}) custom-call(s32[32]{0:T(128)} %reshape.18.ids_ref.refs_0_, s32[32]{0:T(128)} %reshape.19.refs_1_.refs_0_, bf16[32,64,1024]{2,1,0:T(8,128)(2,1)} %all-to-all-done.2.refs_2_, f32[16,98304]{1,0:T(8,128)} %refs_3_.3, ...), custom_call_target="tpu_custom_call" | custom-call | tf_op jit(solution)/shard_map/sophia/pallas_call | solution.py:308
  352.2 33.3 %all-to-all-done.5.refs_1_ = bf16[32,32,1024]{2,1,0:T(8,128)(2,1)S(1)} async-done(((bf16[32,32,1024]{2,1,0:T(8,128)(2,1)}), bf16[32,32,1024]{2,1,0:T(8,128)(2,1)S(1)}, u32[]{:S(2)}, u32[]{:S(2)}) %all-to-all-start.5) | async-done | bytes 2097184 | tf_op jit(solution)/shard_map/all_to_all | solution.py:336
  385.5 0.0 copy-start.1
  385.5 97.7 %all_to_all.41.refs_0_ = bf16[32,64,1024]{2,1,0:T(8,128)(2,1)} all-to-all(bf16[32,64,1024]{2,1,0:T(8,128)(2,1)} %get-tuple-element.25), channel_id=1, replica_groups=mesh['slot'=8,'grp'=4] {'slot','grp'}, dimensions={0} | all-to-all | bytes 8388608 | tf_op jit(solution)/shard_map/all_to_all | solution.py:336
  483.2 0.0 copy-done.1
  483.3 18.5 %slot.3 = (bf16[32,64,1024]{2,1,0:T(8,128)(2,1)}, bf16[32,32,1024]{2,1,0:T(8,128)(2,1)}, bf16[384,1024]{1,0:T(8,128)(2,1)}) custom-call(s32[1]{0:T(128)} %bitcast.count_ref, bf16[2,1,1,384,2048]{4,3,2,1,0:T(8,128)(2,1)} %x_in.3, bf16[2,1,1,384,2048]{4,3,2,1,0:T(8,128)(2,1)} %ct_in.3, bf16[32,64,1024]{2,1,0:T(8,128)(2,1)} %all_to_all.41.refs_0_, ...), custom_call_target="tpu_custom_call" | custom-call | tf_op jit(solution)/shard_map/slot/pallas_call | solution.py:167
  501.7 97.4 %all_to_all.42.refs_2_ = bf16[32,64,1024]{2,1,0:T(8,128)(2,1)} all-to-all(bf16[32,64,1024]{2,1,0:T(8,128)(2,1)} %get-tuple-element.34), channel_id=1, replica_groups=mesh['slot'=8,'grp'=4] {'slot','grp'}, dimensions={0} | all-to-all | bytes 8388608 | tf_op jit(solution)/shard_map/all_to_all | solution.py:336
  599.1 3.8 all-to-all-start.6
  603.0 7.9 %rows.2.refs_2_ = bf16[2,1,1,384,2048]{4,3,2,1,0:T(8,128)(2,1)} custom-call(bf16[384,1024]{1,0:T(8,128)(2,1)} %get-tuple-element.29.dz_ref, bf16[32,32,1024]{2,1,0:T(8,128)(2,1)} %copy-done, bf16[32,64,1024]{2,1,0:T(8,128)(2,1)} %all-to-all-done.1.refs_1_), custom_call_target="tpu_custom_call" | custom-call | tf_op jit(solution)/shard_map/rows/pallas_call | solution.py:198
  610.9 7.8 %rows.3 = bf16[2,1,1,384,2048]{4,3,2,1,0:T(8,128)(2,1)} custom-call(bf16[384,1024]{1,0:T(8,128)(2,1)} %get-tuple-element.28.dz_ref, bf16[32,64,1024]{2,1,0:T(8,128)(2,1)} %all_to_all.41.refs_0_, bf16[32,32,1024]{2,1,0:T(8,128)(2,1)} %copy-done.1, bf16[2,1,1,384,2048]{4,3,2,1,0:T(8,128)(2,1)} %rows.2.refs_2_), custom_call_target="tpu_custom_call", output_to_operand_aliasing={{}: (3, {})} | custom-call | tf_op jit(solution)/shard_map/rows/pallas_call | solution.py:198
  618.6 12.4 %sophia.6 = (f32[16,98304]{1,0:T(8,128)}, f32[16,98304]{1,0:T(8,128)}, f32[16,98304]{1,0:T(8,128)}) custom-call(s32[32]{0:T(128)} %reshape.19.refs_1_.refs_0_, s32[32]{0:T(128)} %reshape.19.refs_1_.refs_0_, bf16[32,64,1024]{2,1,0:T(8,128)(2,1)} %all_to_all.42.refs_2_, f32[16,65536]{1,0:T(8,128)} %get-tuple-element.35.refs_3_, ...), custom_call_target="tpu_custom_call" | custom-call | tf_op jit(solution)/shard_map/sophia/pallas_call | solution.py:308
  631.0 20.5 %all-to-all-done.6.refs_2_ = bf16[32,32,1024]{2,1,0:T(8,128)(2,1)S(1)} async-done(((bf16[32,32,1024]{2,1,0:T(8,128)(2,1)}), bf16[32,32,1024]{2,1,0:T(8,128)(2,1)S(1)}, u32[]{:S(2)}, u32[]{:S(2)}) %all-to-all-start.6) | async-done | bytes 2097184 | tf_op jit(solution)/shard_map/all_to_all | solution.py:336
  651.5 0.0 copy-start.2
  651.5 1.3 copy-done.2
  652.8 7.0 %sophia.7 = (f32[16,98304]{1,0:T(8,128)}, f32[16,98304]{1,0:T(8,128)}, f32[16,98304]{1,0:T(8,128)}) custom-call(s32[32]{0:T(128)} %reshape.19.refs_1_.refs_0_, s32[32]{0:T(128)} %reshape.19.refs_1_.refs_0_, bf16[32,32,1024]{2,1,0:T(8,128)(2,1)} %copy-done.2, ...), custom_call_target="tpu_custom_call", output_to_operand_aliasing={{0}: (6, {}), {1}: (7, {}), {2}: (8, {})} | custom-call | tf_op jit(solution)/shard_map/sophia/pallas_call | solution.py:308
  (1 shorter events, 0.0 us)
Async XLA Ops:
  6.8 56.0 %all-to-all-start = ((bf16[32,32,1024]{2,1,0:T(8,128)(2,1)}), bf16[32,32,1024]{2,1,0:T(8,128)(2,1)S(1)}, u32[]{:S(2)}, u32[]{:S(2)}) async-start(bf16[32,32,1024]{2,1,0:T(8,128)(2,1)} %pack.2), calls=%async_computation | async-start | bytes 4194304 | tf_op jit(solution)/shard_map/all_to_all | solution.py:336
  21.5 45.5 %copy-start.3 = (s32[2,1,1]{0,2,1:T(1,128)S(1)}, s32[2,1,1]{0,2,1:T(1,128)}, u32[]{:S(2)}) copy-start(s32[2,1,1]{0,2,1:T(1,128)} %param.10) | copy-start | bytes 28
  62.9 4.8 copy-start
  62.9 98.4 %all-to-all-start.1 = ((bf16[32,64,1024]{2,1,0:T(8,128)(2,1)}), bf16[32,64,1024]{2,1,0:T(8,128)(2,1)}, u32[]{:S(2)}, u32[]{:S(2)}) async-start(bf16[32,64,1024]{2,1,0:T(8,128)(2,1)} %pack.3), calls=%async_computation.1 | async-start | bytes 8388608 | tf_op jit(solution)/shard_map/all_to_all | solution.py:336
  233.7 98.0 %all-to-all-start.2 = ((bf16[32,64,1024]{2,1,0:T(8,128)(2,1)}), bf16[32,64,1024]{2,1,0:T(8,128)(2,1)}, u32[]{:S(2)}, u32[]{:S(2)}) async-start(bf16[32,64,1024]{2,1,0:T(8,128)(2,1)} %get-tuple-element.24), calls=%async_computation.2 | async-start | bytes 8388608 | tf_op jit(solution)/shard_map/all_to_all | solution.py:336
  331.7 53.8 %all-to-all-start.5 = ((bf16[32,32,1024]{2,1,0:T(8,128)(2,1)}), bf16[32,32,1024]{2,1,0:T(8,128)(2,1)S(1)}, u32[]{:S(2)}, u32[]{:S(2)}) async-start(bf16[32,32,1024]{2,1,0:T(8,128)(2,1)} %get-tuple-element.27), calls=%async_computation.5 | async-start | bytes 4194304 | tf_op jit(solution)/shard_map/all_to_all | solution.py:336
  385.5 97.8 %copy-start.1 = (bf16[32,32,1024]{2,1,0:T(8,128)(2,1)}, bf16[32,32,1024]{2,1,0:T(8,128)(2,1)S(1)}, u32[]{:S(2)}) copy-start(bf16[32,32,1024]{2,1,0:T(8,128)(2,1)S(1)} %all-to-all-done.5.refs_1_) | copy-start | bytes 6291460
  599.1 52.4 %all-to-all-start.6 = ((bf16[32,32,1024]{2,1,0:T(8,128)(2,1)}), bf16[32,32,1024]{2,1,0:T(8,128)(2,1)S(1)}, u32[]{:S(2)}, u32[]{:S(2)}) async-start(bf16[32,32,1024]{2,1,0:T(8,128)(2,1)} %get-tuple-element.30), calls=%async_computation.6 | async-start | bytes 4194304 | tf_op jit(solution)/shard_map/all_to_all | solution.py:336
  651.5 1.3 copy-start.2

commit v4 on v3

--- a/solution.py
+++ b/solution.py
@@ -12,9 +12,6 @@
 WIDE = 2 * FF
 LANES = 128
 TILE = 256
-CHUNKS = 3
-FIRST = ((0, 1), (1, 2))
-REST = ((0, 2), (2, 1))
 
 
 beta_one = 0.9
@@ -162,7 +159,7 @@
 
 def slot_backward(step, spans_in, spans_out, unit, token_rows, cotangents, live_count, arrived):
     devices, cap = arrived[0].shape[0], token_rows.shape[3]
-    rows = devices * CHUNKS * unit
+    rows = devices * unit * sum(count for _, count in spans_in)
     any_spec = pl.BlockSpec(memory_space=pl.ANY)
     out = pl.pallas_call(
         functools.partial(slot_kernel, step, spans_in, spans_out, unit),
@@ -192,7 +189,7 @@
 
 def row_grads(step, spans_in, unit, pre_grad, arrived, shape, before):
     devices, cap = arrived[0].shape[0], pre_grad.shape[0]
-    rows = devices * CHUNKS * unit
+    rows = devices * unit * sum(count for _, count in spans_in)
     kept = [] if before is None else [before]
     any_spec = pl.BlockSpec(memory_space=pl.ANY)
     return pl.pallas_call(
@@ -289,7 +286,7 @@
     )(ids, master)
 
 
-def sophia_chunk(span, unit, ids, next_ids, got, state, whole, final):
+def sophia_chunk(span, unit, ids, next_ids, got, state, whole, width):
     experts, devices = state[0].shape[0], ids.shape[0]
     rows = block_rows(unit)
     chunk_rows = span[1] * unit
@@ -299,7 +296,8 @@
     near = pl.BlockSpec((experts, rows * WIDE), lambda i, *_: (0, i))
     far = pl.BlockSpec((experts, rows * WIDE), lambda i, *_: (0, shift + i))
     packed = pl.BlockSpec((devices, rows, WIDE), lambda i, *_: (0, i, 0))
-    width = unit * CHUNKS * WIDE if final else chunk_rows * WIDE
+    final = width is not None
+    width = width or chunk_rows * WIDE
     out_shape = [jax.ShapeDtypeStruct((experts, width), jnp.float32)] * 3
     out_specs = [far if final else near] * 3
     if not final:
@@ -328,30 +326,34 @@
     device_count = group_count * slot_count
     experts = master.shape[0]
     per_group = experts // group_count
-    unit = master.shape[1] // (CHUNKS * WIDE)
+    share = master.shape[1] // WIDE
+    unit = 16 if share % 16 == 0 else 8
+    parts = share // unit
+    rest = ((0, parts - 1), (parts - 1, 1))
     owners = (jnp.arange(group_count, dtype=jnp.int32) * per_group)[None, :]
     ids = [(place + owners).reshape(-1) for place in (old_place, new_place)]
 
     def swap(array):
         return lax.all_to_all(array, ("slot", "grp"), split_axis=0, concat_axis=0, tiled=True)
 
-    spans = FIRST
+    spans = ((0, 1), (1, parts - 1))
     arrived = [swap(pack_chunk(span, unit, ids[0], master)) for span in spans]
     rows_out = None
-    states = [(momentum, curvature, master)] * len(REST)
+    states = [(momentum, curvature, master)] * len(rest)
     whole = None
     for step in range(2):
         final = step == 1
         grads, pre_grad = slot_backward(
-            step, spans, REST, unit, token_rows, cotangents, row_counts[step, 0], arrived
+            step, spans, rest, unit, token_rows, cotangents, row_counts[step, 0], arrived
         )
         got = [swap(part) for part in grads]
         rows_out = row_grads(
             step, spans, unit, pre_grad, arrived, token_rows.shape, rows_out
         )
-        spans, arrived = REST, []
-        for k, span in enumerate(REST):
-            result = sophia_chunk(span, unit, ids[step], ids[1], got[k], states[k], whole, final)
+        spans, arrived = rest, []
+        for k, span in enumerate(rest):
+            width = master.shape[1] if final else None
+            result = sophia_chunk(span, unit, ids[step], ids[1], got[k], states[k], whole, width)
             if final:
                 whole = tuple(result)
             else:

time: 661 us -> 666 us (level)
  waiting for transfers between devices: 274 us -> 249 us
  blocking collectives: 249 us -> 271 us
  Pallas kernels: 108 us -> 115 us
    all_to_all x5, waiting for transfers between devices: 274 us -> 249 us  [swap(): lax.all_to_all(array, ('slot', 'grp'), split_axis=0, concat_axis=0, tiled...]
    all_to_all x3, blocking collectives: 249 us -> 271 us  [swap(): lax.all_to_all(array, ('slot', 'grp'), split_axis=0, concat_axis=0, tiled...]
  transfers between devices with their start and end apart: 5 -> 5, of which waited for: 5 -> 4; matrix products, arithmetic and copies ran while one was open for 0% -> 0% of each run, Pallas kernels for 9% -> 10%
where the time goes in v4:
time: 666 us; the launch traced here: 665 us
  blocking collectives  271 us (41%)
  waiting for transfers between devices  249 us (37%)
  Pallas kernels  115 us (17%)
  starting transfers between devices  24.1 us (4%)
    all_to_all x3, blocking collectives, swap(): lax.all_to_all(array, ('slot', 'grp'), split_axis=0, concat_axis=0, tiled...  271 us
    all_to_all x5, waiting for transfers between devices, swap(): lax.all_to_all(array, ('slot', 'grp'), split_axis=0, concat_axis=0, tiled...  249 us
    pallas_call x4, Pallas kernels, sophia_chunk(): pl.pallas_call(functools.partial(sophia_kernel, experts, rows, not final,...  49.5 us
    pallas_call x2, Pallas kernels, slot_backward(): pl.pallas_call(functools.partial(slot_kernel, step, spans_in, spans_out,...  37.1 us
    all_to_all x5, starting transfers between devices, swap(): lax.all_to_all(array, ('slot', 'grp'), split_axis=0, concat_axis=0, tiled...  24.1 us
    pallas_call x2, Pallas kernels, row_grads(): pl.pallas_call(functools.partial(rows_kernel, spans_in, unit, len(kept)),...  15.6 us
  transfers between devices with their start and end apart: 5, of which 4 were waited for; matrix products, arithmetic and copies ran while one was open for 0% of the time, Pallas kernels for 10%

profile of v4, /device:TPU:0, one launch (start us, length us, event | category | flops | bytes accessed | tf_op | source)
XLA Modules:
  0.0 664.9 jit_solution(3269783335398455151)
XLA Ops:
  0.6 0.8 broadcast_add_fusion
  1.4 0.1 copy.18
  1.5 0.7 reshape.18.ids_ref.refs_0_
  2.2 3.8 pack.2
  5.9 7.3 %all-to-all-start = ((bf16[32,16,1024]{2,1,0:T(8,128)(2,1)}), bf16[32,16,1024]{2,1,0:T(8,128)(2,1)S(1)}, u32[]{:S(2)}, u32[]{:S(2)}) async-start(bf16[32,16,1024]{2,1,0:T(8,128)(2,1)} %pack.2), calls=%async_computation | async-start | bytes 2097152 | tf_op jit(solution)/shard_map/all_to_all | solution.py:337
  13.3 8.9 %pack.3 = bf16[32,80,1024]{2,1,0:T(8,128)(2,1)} custom-call(s32[32]{0:T(128)} %reshape.18.ids_ref.refs_0_, f32[16,98304]{1,0:T(8,128)} %refs_5_.3), custom_call_target="tpu_custom_call" | custom-call | tf_op jit(solution)/shard_map/pack/pallas_call | solution.py:275
  22.2 0.0 copy-start.3
  22.2 17.3 %all-to-all-done.refs_0_ = bf16[32,16,1024]{2,1,0:T(8,128)(2,1)S(1)} async-done(((bf16[32,16,1024]{2,1,0:T(8,128)(2,1)}), bf16[32,16,1024]{2,1,0:T(8,128)(2,1)S(1)}, u32[]{:S(2)}, u32[]{:S(2)}) %all-to-all-start) | async-done | bytes 1048608 | tf_op jit(solution)/shard_map/all_to_all | solution.py:337
  39.5 0.0 copy-start
  39.5 1.0 copy-done
  40.5 3.7 all-to-all-start.1
  44.2 0.0 copy-done.3
  44.2 0.7 fusion
  44.9 116.3 %all-to-all-done.1.refs_1_ = bf16[32,80,1024]{2,1,0:T(8,128)(2,1)} async-done(((bf16[32,80,1024]{2,1,0:T(8,128)(2,1)}), bf16[32,80,1024]{2,1,0:T(8,128)(2,1)}, u32[]{:S(2)}, u32[]{:S(2)}) %all-to-all-start.1) | async-done | bytes 5242912 | tf_op jit(solution)/shard_map/all_to_all | solution.py:337
  161.2 18.6 %slot.2 = (bf16[32,80,1024]{2,1,0:T(8,128)(2,1)}, bf16[32,16,1024]{2,1,0:T(8,128)(2,1)}, bf16[384,1024]{1,0:T(8,128)(2,1)}) custom-call(s32[1]{0:T(128)} %bitcast.1.count_ref, bf16[2,1,1,384,2048]{4,3,2,1,0:T(8,128)(2,1)} %x_in.3, bf16[2,1,1,384,2048]{4,3,2,1,0:T(8,128)(2,1)} %ct_in.3, bf16[32,16,1024]{2,1,0:T(8,128)(2,1)} %copy-done, ...), custom_call_target="tpu_custom_call" | custom-call | tf_op jit(solution)/shard_map/slot/pallas_call | solution.py:164
  179.8 31.7 %all_to_all.40.refs_2_ = bf16[32,16,1024]{2,1,0:T(8,128)(2,1)} all-to-all(bf16[32,16,1024]{2,1,0:T(8,128)(2,1)} %get-tuple-element.26), channel_id=1, replica_groups=mesh['slot'=8,'grp'=4] {'slot','grp'}, dimensions={0} | all-to-all | bytes 2097152 | tf_op jit(solution)/shard_map/all_to_all | solution.py:337
  211.5 3.7 all-to-all-start.2
  215.2 0.1 copy.19
  215.3 0.7 reshape.19.refs_1_.refs_0_
  216.0 6.7 %sophia.5 = (f32[16,16384]{1,0:T(8,128)}, f32[16,16384]{1,0:T(8,128)}, f32[16,16384]{1,0:T(8,128)}, bf16[32,16,1024]{2,1,0:T(8,128)(2,1)}) custom-call(s32[32]{0:T(128)} %reshape.18.ids_ref.refs_0_, s32[32]{0:T(128)} %reshape.19.refs_1_.refs_0_, bf16[32,16,1024]{2,1,0:T(8,128)(2,1)} %all_to_all.40.refs_2_, f32[16,98304]{1,0:T(8,128)} %refs_3_.3, ...), custom_call_target="tpu_custom_call" | custom-call | tf_op jit(solution)/shard_map/sophia/pallas_call | solution.py:306
  222.7 109.6 %all-to-all-done.2.refs_2_ = bf16[32,80,1024]{2,1,0:T(8,128)(2,1)} async-done(((bf16[32,80,1024]{2,1,0:T(8,128)(2,1)}), bf16[32,80,1024]{2,1,0:T(8,128)(2,1)}, u32[]{:S(2)}, u32[]{:S(2)}) %all-to-all-start.2) | async-done | bytes 5242912 | tf_op jit(solution)/shard_map/all_to_all | solution.py:337
  332.3 5.4 all-to-all-start.5
  337.7 20.6 %sophia.4 = (f32[16,81920]{1,0:T(8,128)}, f32[16,81920]{1,0:T(8,128)}, f32[16,81920]{1,0:T(8,128)}, bf16[32,80,1024]{2,1,0:T(8,128)(2,1)}) custom-call(s32[32]{0:T(128)} %reshape.18.ids_ref.refs_0_, s32[32]{0:T(128)} %reshape.19.refs_1_.refs_0_, bf16[32,80,1024]{2,1,0:T(8,128)(2,1)} %all-to-all-done.2.refs_2_, f32[16,98304]{1,0:T(8,128)} %refs_3_.3, ...), custom_call_target="tpu_custom_call" | custom-call | tf_op jit(solution)/shard_map/sophia/pallas_call | solution.py:306
  358.2 5.6 all-to-all-done.5.refs_1_
  363.9 0.0 copy-start.1
  363.9 119.8 %all_to_all.41.refs_0_ = bf16[32,80,1024]{2,1,0:T(8,128)(2,1)} all-to-all(bf16[32,80,1024]{2,1,0:T(8,128)(2,1)} %get-tuple-element.25), channel_id=1, replica_groups=mesh['slot'=8,'grp'=4] {'slot','grp'}, dimensions={0} | all-to-all | bytes 10485760 | tf_op jit(solution)/shard_map/all_to_all | solution.py:337
  483.7 0.0 copy-done.1
  483.7 18.5 %slot.3 = (bf16[32,80,1024]{2,1,0:T(8,128)(2,1)}, bf16[32,16,1024]{2,1,0:T(8,128)(2,1)}, bf16[384,1024]{1,0:T(8,128)(2,1)}) custom-call(s32[1]{0:T(128)} %bitcast.count_ref, bf16[2,1,1,384,2048]{4,3,2,1,0:T(8,128)(2,1)} %x_in.3, bf16[2,1,1,384,2048]{4,3,2,1,0:T(8,128)(2,1)} %ct_in.3, bf16[32,80,1024]{2,1,0:T(8,128)(2,1)} %all_to_all.41.refs_0_, ...), custom_call_target="tpu_custom_call" | custom-call | tf_op jit(solution)/shard_map/slot/pallas_call | solution.py:164
  502.2 119.9 %all_to_all.42.refs_2_ = bf16[32,80,1024]{2,1,0:T(8,128)(2,1)} all-to-all(bf16[32,80,1024]{2,1,0:T(8,128)(2,1)} %get-tuple-element.34), channel_id=1, replica_groups=mesh['slot'=8,'grp'=4] {'slot','grp'}, dimensions={0} | all-to-all | bytes 10485760 | tf_op jit(solution)/shard_map/all_to_all | solution.py:337
  622.1 3.9 all-to-all-start.6
  626.0 7.8 %rows.2.refs_2_ = bf16[2,1,1,384,2048]{4,3,2,1,0:T(8,128)(2,1)} custom-call(bf16[384,1024]{1,0:T(8,128)(2,1)} %get-tuple-element.29.dz_ref, bf16[32,16,1024]{2,1,0:T(8,128)(2,1)} %copy-done, bf16[32,80,1024]{2,1,0:T(8,128)(2,1)} %all-to-all-done.1.refs_1_), custom_call_target="tpu_custom_call" | custom-call | tf_op jit(solution)/shard_map/rows/pallas_call | solution.py:195
  633.9 7.7 %rows.3 = bf16[2,1,1,384,2048]{4,3,2,1,0:T(8,128)(2,1)} custom-call(bf16[384,1024]{1,0:T(8,128)(2,1)} %get-tuple-element.28.dz_ref, bf16[32,80,1024]{2,1,0:T(8,128)(2,1)} %all_to_all.41.refs_0_, bf16[32,16,1024]{2,1,0:T(8,128)(2,1)} %copy-done.1, bf16[2,1,1,384,2048]{4,3,2,1,0:T(8,128)(2,1)} %rows.2.refs_2_), custom_call_target="tpu_custom_call", output_to_operand_aliasing={{}: (3, {})} | custom-call | tf_op jit(solution)/shard_map/rows/pallas_call | solution.py:195
  641.6 16.5 %sophia.6 = (f32[16,98304]{1,0:T(8,128)}, f32[16,98304]{1,0:T(8,128)}, f32[16,98304]{1,0:T(8,128)}) custom-call(s32[32]{0:T(128)} %reshape.19.refs_1_.refs_0_, s32[32]{0:T(128)} %reshape.19.refs_1_.refs_0_, bf16[32,80,1024]{2,1,0:T(8,128)(2,1)} %all_to_all.42.refs_2_, f32[16,81920]{1,0:T(8,128)} %get-tuple-element.35.refs_3_, ...), custom_call_target="tpu_custom_call" | custom-call | tf_op jit(solution)/shard_map/sophia/pallas_call | solution.py:306
  658.1 0.0 all-to-all-done.6.refs_2_
  658.1 0.0 copy-start.2
  658.1 1.0 copy-done.2
  659.1 5.7 sophia.7
  (1 shorter events, 0.0 us)
Async XLA Ops:
  5.9 33.5 %all-to-all-start = ((bf16[32,16,1024]{2,1,0:T(8,128)(2,1)}), bf16[32,16,1024]{2,1,0:T(8,128)(2,1)S(1)}, u32[]{:S(2)}, u32[]{:S(2)}) async-start(bf16[32,16,1024]{2,1,0:T(8,128)(2,1)} %pack.2), calls=%async_computation | async-start | bytes 2097152 | tf_op jit(solution)/shard_map/all_to_all | solution.py:337
  22.2 22.0 %copy-start.3 = (s32[2,1,1]{0,2,1:T(1,128)S(1)}, s32[2,1,1]{0,2,1:T(1,128)}, u32[]{:S(2)}) copy-start(s32[2,1,1]{0,2,1:T(1,128)} %param.10) | copy-start | bytes 28
  39.5 1.0 copy-start
  40.5 120.8 %all-to-all-start.1 = ((bf16[32,80,1024]{2,1,0:T(8,128)(2,1)}), bf16[32,80,1024]{2,1,0:T(8,128)(2,1)}, u32[]{:S(2)}, u32[]{:S(2)}) async-start(bf16[32,80,1024]{2,1,0:T(8,128)(2,1)} %pack.3), calls=%async_computation.1 | async-start | bytes 10485760 | tf_op jit(solution)/shard_map/all_to_all | solution.py:337
  211.5 120.8 %all-to-all-start.2 = ((bf16[32,80,1024]{2,1,0:T(8,128)(2,1)}), bf16[32,80,1024]{2,1,0:T(8,128)(2,1)}, u32[]{:S(2)}, u32[]{:S(2)}) async-start(bf16[32,80,1024]{2,1,0:T(8,128)(2,1)} %get-tuple-element.24), calls=%async_computation.2 | async-start | bytes 10485760 | tf_op jit(solution)/shard_map/all_to_all | solution.py:337
  332.3 31.6 %all-to-all-start.5 = ((bf16[32,16,1024]{2,1,0:T(8,128)(2,1)}), bf16[32,16,1024]{2,1,0:T(8,128)(2,1)S(1)}, u32[]{:S(2)}, u32[]{:S(2)}) async-start(bf16[32,16,1024]{2,1,0:T(8,128)(2,1)} %get-tuple-element.27), calls=%async_computation.5 | async-start | bytes 2097152 | tf_op jit(solution)/shard_map/all_to_all | solution.py:337
  363.9 119.8 %copy-start.1 = (bf16[32,16,1024]{2,1,0:T(8,128)(2,1)}, bf16[32,16,1024]{2,1,0:T(8,128)(2,1)S(1)}, u32[]{:S(2)}) copy-start(bf16[32,16,1024]{2,1,0:T(8,128)(2,1)S(1)} %all-to-all-done.5.refs_1_) | copy-start | bytes 3145732
  622.1 36.0 %all-to-all-start.6 = ((bf16[32,16,1024]{2,1,0:T(8,128)(2,1)}), bf16[32,16,1024]{2,1,0:T(8,128)(2,1)S(1)}, u32[]{:S(2)}, u32[]{:S(2)}) async-start(bf16[32,16,1024]{2,1,0:T(8,128)(2,1)} %get-tuple-element.30), calls=%async_computation.6 | async-start | bytes 2097152 | tf_op jit(solution)/shard_map/all_to_all | solution.py:337
  658.1 1.0 copy-start.2
